TPU v7x, 32 devices: a whole 2x2x4 slice. The times are simulated.
32 devices in a mesh: seq: 8 (over y, x, core), head: 4 (over z).
Axes of the slice: x: 2, y: 2, z: 4, core: 2. Of those that a mesh axis runs over, the one named last changes fastest.
Arguments:
- tokens: bfloat16 [24576, 768], P(('seq', 'head')), may hold values from -6 to 6
- cotangent: bfloat16 [24576, 768], P(('seq', 'head')), may hold values from -6 to 6
- lengths: int32 [8, 24], P('seq'), may hold values from 1 to 512, 3072 in all within a row
- labels: int32 [8, 24], P('seq'), may hold values from 0 to 2
- w_qkv: bfloat16 [768, 2304], replicated, may hold values from -0.3125 to 0.3125
- b_query: float32 [768], replicated, may hold values from -3 to 3
- b_value: float32 [768], replicated, may hold values from -3 to 3
- w_out: bfloat16 [768, 768], replicated, may hold values from -0.625 to 0.625
- b_out: float32 [768], replicated, may hold values from -3 to 3
- gain_attn: float32 [768], replicated, may hold values from 0.1 to 1.9
- shift_attn: float32 [768], replicated, may hold values from -3 to 3
- w_in: bfloat16 [768, 3072], replicated, may hold values from -0.21875 to 0.21875
- b_in: float32 [3072], replicated, may hold values from -3 to 3
- w_back: bfloat16 [3072, 768], replicated, may hold values from -0.15625 to 0.15625
- b_back: float32 [768], replicated, may hold values from -3 to 3
- gain_ffn: float32 [768], replicated, may hold values from 0.1 to 1.9
- shift_ffn: float32 [768], replicated, may hold values from -3 to 3
- w_pool: bfloat16 [768, 768], replicated, may hold values from -0.21875 to 0.21875
- b_pool: float32 [768], replicated, may hold values from -3 to 3
- w_class: float32 [768, 3], replicated, may hold values from -0.625 to 0.625
Outputs:
- output: bfloat16 [24576, 768], P(('seq', 'head'))
- grad_tokens: float32 [24576, 768], P(('seq', 'head'))
- grad_w_qkv: float32 [768, 2304], P(('seq', 'head'))
- grad_b_query: float32 [768], P(('seq', 'head'))
- grad_b_value: float32 [768], P(('seq', 'head'))
- grad_w_out: float32 [768, 768], P(('seq', 'head'))
- grad_b_out: float32 [768], P(('seq', 'head'))
- grad_gain_attn: float32 [768], P(('seq', 'head'))
- grad_shift_attn: float32 [768], P(('seq', 'head'))
- grad_w_in: float32 [768, 3072], P(('seq', 'head'))
- grad_b_in: float32 [3072], P(('seq', 'head'))
- grad_w_back: float32 [3072, 768], P(('seq', 'head'))
- grad_b_back: float32 [768], P(('seq', 'head'))
- grad_gain_ffn: float32 [768], P(('seq', 'head'))
- grad_shift_ffn: float32 [768], P(('seq', 'head'))
- grad_w_pool: float32 [768, 768], P(('seq', 'head'))
- grad_b_pool: float32 [768], P(('seq', 'head'))
- grad_w_class: float32 [768, 3], P(('seq', 'head'))
- entropy: float32 [], replicated
Inputs may be any that keep to these rules, and one draw needn't show every extreme that they name: Each row of 24 lengths sums to 3072, and its largest length is 512.
All inputs are finite; a program needn't handle non-finite values.
Results may differ from a plain program's by a relative error of at most 0.014.
The roundings to bfloat16 on the way count: a program that leaves them out, or rounds other values in their place, can miss the bound.
Values may be sent and summed in bfloat16 or wider, within the bound.
A program may use at most 192 MiB of HBM per device.

v0:
```python
import functools

import jax
import jax.numpy as jnp
from jax import lax
from jax.experimental import pallas as pl
from jax.experimental.pallas import tpu as pltpu
from jax.sharding import PartitionSpec as P

HEAD_DIM = 64
MAXLEN = 512
PAIR = 2 * HEAD_DIM
QBLK = 128
KCHUNK = 256
PAD = KCHUNK - 128
LSE0 = 32
SIDE = 128

eps = 1e-05
BIG = 1e30
highest = lax.Precision.HIGHEST
f32 = jnp.float32
bf16 = jnp.bfloat16
NT = (((1,), (1,)), ((), ()))
NN = (((1,), (0,)), ((), ()))
TN = (((0,), (0,)), ((), ()))


def dot(left, right, dims):
    return lax.dot_general(left, right, dims, preferred_element_type=f32)


def pair_rows(rows, side):
    lane = lax.broadcasted_iota(jnp.int32, rows.shape, 1)
    zero = jnp.zeros_like(rows)
    first = jnp.where(lane < HEAD_DIM, rows, zero)
    second = jnp.where(lane >= HEAD_DIM, rows, zero)
    return jnp.concatenate(
        [jnp.concatenate([first, side[0]], axis=1), jnp.concatenate([second, side[1]], axis=1)],
        axis=0,
    )


def unpair(both):
    row = lax.broadcasted_iota(jnp.int32, (PAIR, QBLK), 0)
    return jnp.where(row < HEAD_DIM, both[:, :QBLK], both[:, QBLK:])


def attend_kernel(bounds, q_ref, k_ref, v_ref, hot_ref, mask_ref, ctx_ref, lse_ref, kcat, vt):
    window = k_ref.shape[0]
    own = ctx_ref.shape[0]
    fold = kcat.shape[0]
    skip = MAXLEN // QBLK

    @pl.when(pl.program_id(0) == 0)
    def _():
        for j in range(fold):
            kcat[j, :, PAIR:] = mask_ref[...]
            kcat[j, pl.ds(window, PAD), :PAIR] = jnp.zeros((PAD, PAIR), bf16)
            vt[j, :, pl.ds(window, PAD)] = jnp.zeros((PAIR, PAD), bf16)

    lse_ref[...] = jnp.zeros_like(lse_ref)
    for j in range(fold):
        cols = pl.ds(j * PAIR, PAIR)
        kcat[j, pl.ds(0, window), :PAIR] = k_ref[:, cols]
        for at in range(0, window, 256):
            vt[j, :, pl.ds(at, 256)] = v_ref[pl.ds(at, 256), cols].T

    def block(i, carry):
        row0 = pl.multiple_of(i * QBLK, QBLK)
        hot = hot_ref[pl.ds(MAXLEN + row0, QBLK), :]
        rows = q_ref[pl.ds(MAXLEN + row0, QBLK), :]
        qcat = [pair_rows(rows[:, j * PAIR : (j + 1) * PAIR], (hot, hot)) for j in range(fold)]
        first = bounds[skip + i, 0]

        def step(c, state):
            start = pl.multiple_of(first + c * KCHUNK, 128)
            scores = [dot(kcat[j, pl.ds(start, KCHUNK), :], qcat[j], NT) for j in range(fold)]
            out = []
            for j, s in enumerate(scores):
                peak, total, acc = state[j]
                new_peak = jnp.maximum(peak, jnp.max(s, axis=0, keepdims=True))
                scale = jnp.exp(peak - new_peak)
                p = jnp.exp(s - new_peak)
                total = total * scale + jnp.sum(p, axis=0, keepdims=True)
                acc = acc * scale + dot(vt[j, :, pl.ds(start, KCHUNK)], p.astype(bf16), NN)
                out.append((new_peak, total, acc))
            return tuple(out)

        empty = (
            jnp.full((1, 2 * QBLK), -BIG, f32),
            jnp.zeros((1, 2 * QBLK), f32),
            jnp.zeros((PAIR, 2 * QBLK), f32),
        )
        state = lax.fori_loop(0, bounds[skip + i, 1], step, (empty,) * fold)
        for j, (peak, total, acc) in enumerate(state):
            ctx_ref[pl.ds(row0, QBLK), pl.ds(j * PAIR, PAIR)] = unpair(acc / total).T.astype(bf16)
            lse = peak + jnp.log(total)
            lse_ref[2 * j : 2 * j + 1, pl.ds(row0, QBLK)] = lse[:, :QBLK]
            lse_ref[2 * j + 1 : 2 * j + 2, pl.ds(row0, QBLK)] = lse[:, QBLK:]
        return carry

    lax.fori_loop(0, own // QBLK, block, 0)


def fold_of(pairs, most):
    return max(n for n in range(1, most + 1) if pairs % n == 0)


def attend(bounds, qkv, hot, mask, own):
    window, wide = qkv.shape
    width = wide // 3
    pairs = width // PAIR
    fold = fold_of(pairs, 3)
    parts = pairs // fold
    column = lambda part: pl.BlockSpec((window, fold * PAIR), lambda g, b: (0, part * parts + g))
    whole = lambda a: pl.BlockSpec(a.shape, lambda g, b: (0, 0))
    return pl.pallas_call(
        attend_kernel,
        grid_spec=pltpu.PrefetchScalarGridSpec(
            num_scalar_prefetch=1,
            grid=(parts,),
            in_specs=[column(0), column(1), column(2), whole(hot), whole(mask)],
            out_specs=[
                pl.BlockSpec((own, fold * PAIR), lambda g, b: (0, g)),
                pl.BlockSpec((8, own), lambda g, b: (g, 0)),
            ],
            scratch_shapes=[
                pltpu.VMEM((fold, window + PAD, 2 * PAIR), bf16),
                pltpu.VMEM((fold, PAIR, window + PAD), bf16),
            ],
        ),
        out_shape=[
            jax.ShapeDtypeStruct((own, width), bf16),
            jax.ShapeDtypeStruct((8 * parts, own), f32),
        ],
        cost_estimate=pl.CostEstimate(
            flops=own * 600 * width * 4, bytes_accessed=window * wide * 2, transcendentals=0
        ),
        name="attend",
    )(bounds, qkv, qkv, qkv, hot, mask)


def attend_back_kernel(side0, more, bounds, q_ref, k_ref, v_ref, do_ref, side_ref, hot_ref, mask_ref, *refs):
    extra, refs = refs[:more], refs[more:]
    gqkv_ref, (kcat, vcat, kt, dk, dv) = refs[0], refs[-5:]
    window = k_ref.shape[0]
    own = gqkv_ref.shape[1]
    fold = kcat.shape[0]
    low0, gap = side0

    for j in range(fold):
        cols = pl.ds(j * PAIR, PAIR)
        kcat[j, :, PAIR:] = mask_ref[...]
        vcat[j, :, PAIR:] = jnp.ones((window + PAD, SIDE), bf16)
        kcat[j, pl.ds(window, PAD), :PAIR] = jnp.zeros((PAD, PAIR), bf16)
        vcat[j, pl.ds(window, PAD), :PAIR] = jnp.zeros((PAD, PAIR), bf16)
        kt[j, :, pl.ds(window, PAD)] = jnp.zeros((PAIR, PAD), bf16)
        kcat[j, pl.ds(0, window), :PAIR] = k_ref[:, cols]
        vcat[j, pl.ds(0, window), :PAIR] = v_ref[:, cols]
        for at in range(0, window, 256):
            kt[j, :, pl.ds(at, 256)] = k_ref[pl.ds(at, 256), cols].T
    dk[...] = jnp.zeros_like(dk)
    dv[...] = jnp.zeros_like(dv)
    lane = lax.broadcasted_iota(jnp.int32, (QBLK, SIDE), 1)

    def side_lanes(side, first):
        return jnp.where((lane >= first) & (lane < first + 3), side, jnp.zeros_like(side))

    def block(i, carry):
        row0 = pl.multiple_of(i * QBLK, QBLK)
        hot = hot_ref[pl.ds(row0, QBLK), :]
        side = side_ref[pl.ds(row0, QBLK), :]
        rows = q_ref[pl.ds(row0, QBLK), :]
        grads = do_ref[pl.ds(row0, QBLK), :]
        qcat, docat = [], []
        for j in range(fold):
            cols = slice(j * PAIR, (j + 1) * PAIR)
            low = low0 + 6 * j
            qcat.append(
                pair_rows(
                    rows[:, cols],
                    (hot + side_lanes(side, low), hot + side_lanes(side, low + 3)),
                )
            )
            docat.append(
                pair_rows(
                    grads[:, cols],
                    (side_lanes(side, low + gap), side_lanes(side, low + gap + 3)),
                )
            )
        first = bounds[i, 0]

        def step(c, dq):
            start = pl.multiple_of(first + c * KCHUNK, 128)
            here = pl.ds(start, KCHUNK)
            scores = [dot(kcat[j, here, :], qcat[j], NT) for j in range(fold)]
            slopes = [dot(vcat[j, here, :], docat[j], NT) for j in range(fold)]
            out = []
            for j in range(fold):
                p = jnp.exp(scores[j])
                ds = (p * slopes[j]).astype(bf16)
                dv[j, here, :] += dot(p.astype(bf16), docat[j][:, :PAIR], NN)
                dk[j, here, :] += dot(ds, qcat[j][:, :PAIR], NN)
                out.append(dq[j] + dot(kt[j, :, here], ds, NN))
            return tuple(out)

        dq = lax.fori_loop(
            0, bounds[i, 1], step, (jnp.zeros((PAIR, 2 * QBLK), f32),) * fold
        )

        @pl.when((i >= MAXLEN // QBLK) & (i < (MAXLEN + own) // QBLK))
        def _():
            for j in range(fold):
                gqkv_ref[
                    0, pl.ds(pl.multiple_of(row0 - MAXLEN, QBLK), QBLK), pl.ds(j * PAIR, PAIR)
                ] = (unpair(dq[j]) * HEAD_DIM**-0.5).T.astype(bf16)

        return carry

    lax.fori_loop(0, window // QBLK, block, 0)
    for j in range(fold):
        cols = pl.ds(j * PAIR, PAIR)
        gqkv_ref[1, :, cols] = dk[j, pl.ds(MAXLEN, own), :].astype(bf16)
        gqkv_ref[2, :, cols] = dv[j, pl.ds(MAXLEN, own), :].astype(bf16)

    if more:
        tok_t, place = extra[:2]
        keep, send, sums = refs[1:4]
        sums[...] = jnp.zeros_like(sums)

        def third(n, carry):
            grads = gqkv_ref[n]
            sums[pl.ds(n, 1), :] = col_sum(grads.astype(f32))
            mine, theirs = halves(dot(tok_t[...], grads, NN), place[0], keep.shape[2])
            for g in range(len(mine)):
                keep[n, g] = mine[g]
                send[n, g] = theirs[g]
            return carry

        lax.fori_loop(0, 3, third, 0)


def attend_back(part, fold, bounds, qkv, grads, hot, mask, own, extra=()):
    window, wide = qkv.shape
    width = wide // 3
    pairs = width // PAIR
    parts = pairs // fold
    column = lambda c: pl.BlockSpec((window, fold * PAIR), lambda g, b: (0, c * parts + part))
    whole = lambda a: pl.BlockSpec(a.shape, lambda g, b: (0, 0))
    side0 = (LSE0 + 6 * fold * part, 6 * pairs)
    shape = jax.ShapeDtypeStruct
    cols = fold * PAIR
    more_in, more_out = [], []
    if extra:
        more_in = [whole(extra[0]), pl.BlockSpec(memory_space=pltpu.SMEM)]
        more_out = [shape((3, 4, width // 8, cols), bf16)] * 2 + [shape((8, cols), f32)]
    block = lambda a: pl.BlockSpec(a.shape, lambda g, b: (0,) * len(a.shape))
    outs = [shape((3, own, cols), bf16)] + more_out
    results = pl.pallas_call(
        functools.partial(attend_back_kernel, side0, len(extra)),
        grid_spec=pltpu.PrefetchScalarGridSpec(
            num_scalar_prefetch=1,
            grid=(1,),
            in_specs=[
                column(0),
                column(1),
                column(2),
                pl.BlockSpec((window, fold * PAIR), lambda g, b: (0, part)),
                pl.BlockSpec((window, SIDE), lambda g, b: (0, pairs)),
                whole(hot),
                whole(mask),
            ]
            + more_in,
            out_specs=[block(o) for o in outs],
            scratch_shapes=[
                pltpu.VMEM((fold, window + PAD, 2 * PAIR), bf16),
                pltpu.VMEM((fold, window + PAD, 2 * PAIR), bf16),
                pltpu.VMEM((fold, PAIR, window + PAD), bf16),
                pltpu.VMEM((fold, window + PAD, PAIR), f32),
                pltpu.VMEM((fold, window + PAD, PAIR), f32),
            ],
        ),
        out_shape=outs,
        cost_estimate=pl.CostEstimate(
            flops=own * 900 * PAIR * fold * 16,
            bytes_accessed=window * PAIR * fold * 8,
            transcendentals=0,
        ),
        name=f"attend_back{part}",
    )(bounds, qkv, qkv, qkv, grads, grads, hot, mask, *extra)
    return results if extra else results[0]


def low3(values):
    high = values.astype(bf16)
    rest = values - high.astype(f32)
    mid = rest.astype(bf16)
    return high, mid, (rest - mid.astype(f32)).astype(bf16)


def dot3(values, chosen, dims):
    return sum(dot(part, chosen, dims) for part in low3(values))


def iota(shape, axis):
    return lax.broadcasted_iota(jnp.int32, shape, axis)


def mean_row(values):
    return jnp.mean(values, axis=-1, keepdims=True)


def col_sum(values):
    return jnp.sum(values, axis=0, keepdims=True)


def norm_back(grad_out, normed, inv_std, gain_vec):
    grad_norm = grad_out * gain_vec
    inner = grad_norm - mean_row(grad_norm) - normed * mean_row(grad_norm * normed)
    return inv_std * inner, col_sum(grad_out * normed), col_sum(grad_out)


ROWS = 256
VECTORS = 24


def middle_kernel(
    heads_part, place, w_in_hbm, w_back_hbm, w_pool_hbm, tok, ctx, lse, cot, w_out, b_in, w_class, small, seqs_of,
    out, gar, gs, act_hbm, gpre_hbm, gffn, mid, gattn, cls, gpool, vec,
    w_in, w_back, w_pool, act, gpre, slope, unit_a, unit_f, inv_a, inv_f, acc, sems,
):
    own, width = tok.shape
    b_out, gain_a, shift_a, b_back, gain_f, shift_f, b_pool = (small[n : n + 1, :] for n in range(7))
    starts, labels = seqs_of[:, 0:1], seqs_of[:, 1:2]
    chunks, _, wide = act.shape
    blocks = own // ROWS
    n_class = w_class.shape[0]
    loads = [
        pltpu.make_async_copy(w_in_hbm, w_in, sems.at[0]),
        pltpu.make_async_copy(w_back_hbm, w_back, sems.at[1]),
        pltpu.make_async_copy(w_pool_hbm, w_pool, sems.at[2]),
    ]
    for load in loads:
        load.start()

    def at(b):
        return pl.ds(pl.multiple_of(b * ROWS, ROWS), ROWS)

    def cols(c):
        return pl.ds(pl.multiple_of(c * wide, wide), wide)

    def norm(hidden, rows, unit, inv, gain, shift):
        centred = hidden - mean_row(hidden)
        inv_std = lax.rsqrt(mean_row(centred * centred) + eps)
        normed = centred * inv_std
        unit[rows, :] = normed
        inv[rows, :] = inv_std
        return (normed * gain[...] + shift[...]).astype(bf16)

    def first_norm(b, carry):
        rows = at(b)
        hidden = tok[rows, :].astype(f32) + dot(ctx[rows, :], w_out[...], NN) + b_out[...]
        mid[rows, :] = norm(hidden, rows, unit_a, inv_a, gain_a, shift_a)
        return carry

    lax.fori_loop(0, blocks, first_norm, 0)
    loads[0].wait()
    loads[1].wait()
    acc[...] = jnp.zeros_like(acc)

    def forward(c, carry):
        for b in range(blocks):
            rows = slice(b * ROWS, (b + 1) * ROWS)
            pre = dot(mid[rows, :], w_in[:, cols(c)], NN) + b_in[:, cols(c)]
            cdf = 0.5 * (1.0 + lax.erf(pre * (0.5**0.5)))
            low = (pre * cdf).astype(bf16)
            act[c, rows, :] = low
            slope[c, rows, :] = cdf + pre * (jnp.exp(-0.5 * pre * pre) * 0.3989422804014327)
            acc[rows, :] += dot(low, w_back[cols(c), :], NN)
        pltpu.make_async_copy(act.at[c], act_hbm.at[c], sems.at[3 + c]).start()
        return carry

    lax.fori_loop(0, chunks, forward, 0)

    def second_norm(b, carry):
        rows = at(b)
        hidden = mid[rows, :].astype(f32) + (acc[rows, :] + b_back[...])
        out[rows, :] = norm(hidden, rows, unit_f, inv_f, gain_f, shift_f)
        return carry

    lax.fori_loop(0, blocks, second_norm, 0)

    loads[2].wait()
    seqs = starts.shape[0]
    picked = (iota((seqs, own), 1) + place[0] * own == starts[...]).astype(f32)
    sel = picked.astype(bf16)
    owned = jnp.sum(picked, axis=1, keepdims=True)
    cls_low = dot(sel, out[...], NN).astype(bf16)
    cls[...] = cls_low
    pooled = jnp.tanh(dot(cls_low, w_pool[...], NN) + b_pool[...])
    logits = [jnp.sum(pooled * w_class[c : c + 1, :], axis=1, keepdims=True) for c in range(n_class)]
    peak = functools.reduce(jnp.maximum, logits)
    expo = [jnp.exp(x - peak) for x in logits]
    total = sum(expo)
    probs = [x / total for x in expo]
    terms = owned * (peak + jnp.log(total) - sum(p * x for p, x in zip(probs, logits)))
    entropy = jnp.sum(terms, axis=0, keepdims=True)
    g_logits = [
        (probs[c] - (labels[...] == c).astype(f32)) * owned for c in range(n_class)
    ]
    g_pooled = sum(g_logits[c] * w_class[c : c + 1, :] for c in range(n_class))
    g_low = (g_pooled * (1.0 - pooled * pooled)).astype(bf16)
    gpool[...] = g_low
    grad_cls = dot(g_low, w_pool[...], NT)

    def second_back(b, carry):
        rows = at(b)
        here = (
            iota((seqs, ROWS), 1) + (place[0] * own + b * ROWS) == starts[...]
        ).astype(f32).astype(bf16)
        back = sum(dot(here, part, TN) for part in low3(grad_cls))
        grad_out = cot[rows, :].astype(f32) + back
        res, g_gain, g_shift = norm_back(grad_out, unit_f[rows, :], inv_f[rows, :], gain_f[...])
        low = res.astype(bf16)
        gar[rows, :] = res
        gffn[rows, :] = low
        return carry[0] + g_gain, carry[1] + g_shift, carry[2] + col_sum(low.astype(f32))

    zero = jnp.zeros((1, width), f32)
    sums_f = lax.fori_loop(0, blocks, second_back, (zero, zero, zero))
    acc[...] = jnp.zeros_like(acc)

    def backward(c, carry):
        g_b_in = jnp.zeros((1, wide), f32)
        for b in range(blocks):
            rows = slice(b * ROWS, (b + 1) * ROWS)
            grad_act = dot(gffn[rows, :], w_back[cols(c), :], NT)
            low = (grad_act * slope[c, rows, :]).astype(bf16)
            gpre[c, rows, :] = low
            g_b_in += col_sum(low.astype(f32))
            acc[rows, :] += dot(low, w_in[:, cols(c)], NT)
        vec[pl.ds(8 + c, 1), :] = g_b_in
        pltpu.make_async_copy(gpre.at[c], gpre_hbm.at[c], sems.at[3 + chunks + c]).start()
        return carry

    lax.fori_loop(0, chunks, backward, 0)

    heads = width // HEAD_DIM
    lane = iota((1, SIDE), 1)
    gap = LSE0 + 3 * heads
    feature, flane = iota((width, SIDE), 0), iota((width, SIDE), 1)
    third = flane - gap - 3 * (feature // HEAD_DIM)
    head_sum = ((third >= 0) & (third < 3)).astype(f32).astype(bf16)
    lrow, llane = iota((lse.shape[0], SIDE), 0), iota((lse.shape[0], SIDE), 1)
    lhead = (lrow // 8) * heads_part + lrow % 8
    spread = [
        ((llane == LSE0 + 3 * lhead + p) & (lrow % 8 < heads_part)).astype(f32).astype(bf16)
        for p in range(3)
    ]
    which = lax.rem(lane - gap + 3 * heads, 3)

    def first_back(b, carry):
        rows = at(b)
        grad_mid = gar[rows, :] + acc[rows, :]
        res, g_gain, g_shift = norm_back(grad_mid, unit_a[rows, :], inv_a[rows, :], gain_a[...])
        low = res.astype(bf16)
        gar[rows, :] = res
        gattn[rows, :] = low
        grad_ctx = dot(low, w_out[...], NT).astype(bf16)
        gs[rows, :width] = grad_ctx
        delta = dot3(grad_ctx.astype(f32) * ctx[rows, :].astype(f32), head_sum, NN)
        high, mid_part, rest = low3(-delta)
        side = jnp.where(which == 0, high, jnp.where(which == 1, mid_part, rest))
        lse_parts = low3(-lse[:, rows])
        side_lse = sum(dot(part, spread[p], TN) for p, part in enumerate(lse_parts))
        gs[rows, width:] = side + side_lse.astype(bf16)
        return carry[0] + g_gain, carry[1] + g_shift, carry[2] + col_sum(low.astype(f32))

    sums_a = lax.fori_loop(0, blocks, first_back, (zero, zero, zero))
    for row, value in enumerate((sums_a[2], sums_a[0], sums_a[1], sums_f[2], sums_f[0], sums_f[1])):
        vec[row : row + 1, :] = value
    vec[6:7, :] = col_sum(g_low.astype(f32))
    vec[7:8, :] = jnp.broadcast_to(entropy, (1, width))
    for c in range(n_class):
        vec[8 + chunks + c : 9 + chunks + c, :] = col_sum(pooled * g_logits[c])
    done = 8 + chunks + n_class
    vec[done:, :] = jnp.zeros((VECTORS - done, width), f32)
    for c in range(chunks):
        pltpu.make_async_copy(act.at[c], act_hbm.at[c], sems.at[3 + c]).wait()
        pltpu.make_async_copy(gpre.at[c], gpre_hbm.at[c], sems.at[3 + chunks + c]).wait()


def middle_layer(heads_part, place, w_in, w_back, w_pool, tok, ctx, lse, cot, w_out, b_in, w_class, small, seqs_of):
    own, width = tok.shape
    ff = w_in.shape[1]
    chunks = ff // width
    seqs = seqs_of.shape[0]
    vmem = pl.BlockSpec(memory_space=pltpu.VMEM)
    hbm = pl.BlockSpec(memory_space=pl.ANY)
    shape = jax.ShapeDtypeStruct
    flops = 2 * own * width * (6 * width + 4 * ff)
    return pl.pallas_call(
        functools.partial(middle_kernel, heads_part),
        in_specs=[pl.BlockSpec(memory_space=pltpu.SMEM), hbm, hbm, hbm] + [vmem] * 9,
        out_specs=[vmem, vmem, vmem, hbm, hbm] + [vmem] * 6,
        out_shape=[
            shape((own, width), bf16),
            shape((own, width), f32),
            shape((own, width + SIDE), bf16),
            shape((chunks, own, width), bf16),
            shape((chunks, own, width), bf16),
            shape((own, width), bf16),
            shape((own, width), bf16),
            shape((own, width), bf16),
            shape((seqs, width), bf16),
            shape((seqs, width), bf16),
            shape((VECTORS, width), f32),
        ],
        scratch_shapes=[
            pltpu.VMEM(w_in.shape, bf16),
            pltpu.VMEM(w_back.shape, bf16),
            pltpu.VMEM(w_pool.shape, bf16),
            pltpu.VMEM((chunks, own, width), bf16),
            pltpu.VMEM((chunks, own, width), bf16),
            pltpu.VMEM((chunks, own, width), f32),
            pltpu.VMEM((own, width), f32),
            pltpu.VMEM((own, width), f32),
            pltpu.VMEM((own, 1), f32),
            pltpu.VMEM((own, 1), f32),
            pltpu.VMEM((own, width), f32),
            pltpu.SemaphoreType.DMA((3 + 2 * chunks,)),
        ],
        compiler_params=pltpu.CompilerParams(vmem_limit_bytes=62 * 2**20),
        cost_estimate=pl.CostEstimate(flops=flops, bytes_accessed=30 * 2**20, transcendentals=0),
        name="middle_layer",
    )(place, w_in, w_back, w_pool, tok, ctx, lse, cot, w_out, b_in, w_class, small, seqs_of)


def split_core(tile, core, half, keep, send, first):
    for n in range(tile.shape[0] // (2 * half)):
        even = tile[2 * n * half : (2 * n + 1) * half, :]
        odd = tile[(2 * n + 1) * half : (2 * n + 2) * half, :]
        keep[first + n, :, :] = jnp.where(core == 0, even, odd).astype(bf16)
        send[first + n, :, :] = jnp.where(core == 0, odd, even).astype(bf16)


def weight_grads_kernel(
    core, act, gpre, gffn, mid, ctx, gattn, cls, gpool,
    back_keep, back_send, in_keep, in_send, out_keep, out_send, mid_t,
):
    y = pl.program_id(0)

    @pl.when(y == 0)
    def _():
        mid_t[...] = mid[...].T
        split_core(dot(ctx[...], gattn[...], TN), core[0], out_keep.shape[1], out_keep, out_send, 0)

    @pl.when(y == 1)
    def _():
        split_core(dot(cls[...], gpool[...], TN), core[0], out_keep.shape[1], out_keep, out_send, 0)

    split_core(dot(act[0], gffn[...], TN), core[0], back_keep.shape[1], back_keep, back_send, 0)
    split_core(dot(mid_t[...], gpre[0], NN), core[0], in_keep.shape[1], in_keep, in_send, 0)


def weight_grads(core, n_seq, act, gpre, gffn, mid, ctx, gattn, cls, gpool):
    chunks, own, width = act.shape
    groups = n_seq // 2
    half_b, half_w = chunks * width // n_seq, width // n_seq
    shape = jax.ShapeDtypeStruct
    whole = lambda a: pl.BlockSpec(a.shape, lambda y, c: (0, 0))
    tile = pl.BlockSpec((1, own, width), lambda y, c: (y, 0, 0))
    back = pl.BlockSpec((groups // chunks, half_b, width), lambda y, c: (y, 0, 0))
    inner = pl.BlockSpec((groups, half_w, width), lambda y, c: (0, 0, y))
    outer = pl.BlockSpec((groups, half_w, width), lambda y, c: (0, 0, jnp.minimum(y, 1)))
    return pl.pallas_call(
        weight_grads_kernel,
        grid_spec=pltpu.PrefetchScalarGridSpec(
            num_scalar_prefetch=1,
            grid=(chunks,),
            in_specs=[tile, tile] + [whole(a) for a in (gffn, mid, ctx, gattn, cls, gpool)],
            out_specs=[back, back, inner, inner, outer, outer],
            scratch_shapes=[pltpu.VMEM((width, own), bf16)],
        ),
        out_shape=[shape((groups, half_b, width), bf16)] * 2
        + [shape((groups, half_w, chunks * width), bf16)] * 2
        + [shape((groups, half_w, 2 * width), bf16)] * 2,
        compiler_params=pltpu.CompilerParams(vmem_limit_bytes=48 * 2**20),
        cost_estimate=pl.CostEstimate(
            flops=2 * own * width * width * (2 * chunks + 1), bytes_accessed=30 * 2**20, transcendentals=0
        ),
        name="weight_grads",
    )(core, act, gpre, gffn, mid, ctx, gattn, cls, gpool)


def last_kernel(n_parts, core, *refs):
    tok, gar, w_qkv = refs[:3]
    parts = refs[3 : 3 + n_parts]
    gtok, vec = refs[3 + n_parts : 5 + n_parts]
    pairs = refs[5 + n_parts : 11 + n_parts]
    tok_t = refs[11 + n_parts]
    c = pl.program_id(0)

    @pl.when(c == 0)
    def _():
        tok_t[...] = tok[...].T
        gtok[...] = gar[...]
        vec[...] = jnp.zeros_like(vec)

    grads = jnp.concatenate([p[0] for p in parts], axis=1)
    gtok[...] += dot(grads, w_qkv[...], NT)
    vec[pl.ds(c, 1), :] = col_sum(grads.astype(f32))
    tile = dot(tok_t[...], grads, NN)
    for n in range(3):

        @pl.when(c == n)
        def _():
            keep, send = pairs[2 * n], pairs[2 * n + 1]
            split_core(tile, core[0], keep.shape[1], keep, send, 0)


def last_layer(core, n_seq, tok, gar, w_qkv, parts):
    own, width = tok.shape
    groups, half = n_seq // 2, width // n_seq
    shape = jax.ShapeDtypeStruct
    whole = lambda a: pl.BlockSpec(a.shape, lambda c, k: (0,) * len(a.shape))
    pair = pl.BlockSpec((groups, half, width), lambda c, k: (0, 0, 0))
    return pl.pallas_call(
        functools.partial(last_kernel, len(parts)),
        grid_spec=pltpu.PrefetchScalarGridSpec(
            num_scalar_prefetch=1,
            grid=(3,),
            in_specs=[whole(tok), whole(gar), pl.BlockSpec((width, width), lambda c, k: (0, c))]
            + [pl.BlockSpec((1,) + p.shape[1:], lambda c, k: (c, 0, 0)) for p in parts],
            out_specs=[whole(gar), pl.BlockSpec((8, width), lambda c, k: (0, 0))] + [pair] * 6,
            scratch_shapes=[pltpu.VMEM((width, own), bf16)],
        ),
        out_shape=[shape((own, width), f32), shape((8, width), f32)]
        + [shape((groups, half, width), bf16)] * 6,
        compiler_params=pltpu.CompilerParams(vmem_limit_bytes=40 * 2**20),
        cost_estimate=pl.CostEstimate(
            flops=12 * own * width * width, bytes_accessed=12 * 2**20, transcendentals=0
        ),
        name="last_layer",
    )(core, tok, gar, w_qkv, *parts)


MESH = pl.DeviceIdType.MESH
OTHER_CORE, NEAR = 1, (2, 4, 6)


class Sends:
    def __init__(self, send_sems, recv_sems):
        self.sems, self.copies, self.at = (send_sems, recv_sems), {}, 0

    def plan(self, name, src, dst, **device):
        self.copies[name] = pltpu.make_async_remote_copy(
            src_ref=src,
            dst_ref=dst,
            send_sem=self.sems[0].at[self.at],
            recv_sem=self.sems[1].at[self.at],
            device_id=device,
            device_id_type=MESH,
        )
        self.at += 1

    def start(self, *names):
        for name in names:
            self.copies[name].start()

    def arrived(self, *names):
        for name in names:
            self.copies[name].wait_recv()

    def drain(self):
        for copy in self.copies.values():
            copy.wait_send()


def greet(devices):
    barrier = pltpu.get_barrier_semaphore()
    for device in devices:
        pl.semaphore_signal(barrier, inc=1, device_id=device, device_id_type=MESH)
    pl.semaphore_wait(barrier, len(devices))


def halves(tile, core, half):
    even = [tile[2 * n * half : (2 * n + 1) * half] for n in range(tile.shape[0] // (2 * half))]
    odd = [tile[(2 * n + 1) * half : (2 * n + 2) * half] for n in range(tile.shape[0] // (2 * half))]
    keep = [jnp.where(core == 0, e, o).astype(bf16) for e, o in zip(even, odd)]
    send = [jnp.where(core == 0, o, e).astype(bf16) for e, o in zip(even, odd)]
    return keep, send


def front_kernel(
    tok, w_hbm, small, lens, labels, qkv_hbm, hot, mask, bounds, seqs_of,
    sides, w, work, rows_of, load_sem, out_sems, send_sems, recv_sems,
):
    head, n_head = lax.axis_index("head"), lax.axis_size("head")
    own, width = tok.shape
    window = hot.shape[0]
    load = pltpu.make_async_copy(w_hbm, w, load_sem)
    load.start()
    not_first, not_last = head > 0, head < n_head - 1
    barrier = pltpu.get_barrier_semaphore()

    @pl.when(not_first)
    def _():
        pl.semaphore_signal(barrier, inc=1, device_id={"head": head - 1}, device_id_type=MESH)

    @pl.when(not_last)
    def _():
        pl.semaphore_signal(barrier, inc=1, device_id={"head": head + 1}, device_id_type=MESH)

    pl.semaphore_wait(barrier, not_first.astype(jnp.int32) + not_last.astype(jnp.int32))
    pieces = MAXLEN // ROWS
    here = lambda n: pl.ds(n * ROWS, ROWS)
    up, down = [], []
    for n in range(pieces):
        for copies, first, side, device in (
            (up, own - MAXLEN, 0, lax.rem(head + 1, n_head)),
            (down, 0, 1, lax.rem(head + n_head - 1, n_head)),
        ):
            copies.append(
                pltpu.make_async_remote_copy(
                    src_ref=tok.at[pl.ds(first + n * ROWS, ROWS)], dst_ref=sides.at[side, here(n)],
                    send_sem=send_sems.at[side, n], recv_sem=recv_sems.at[side, n],
                    device_id={"head": device}, device_id_type=MESH,
                )
            )

    @pl.when(not_last)
    def _():
        for copy in up:
            copy.start()

    @pl.when(not_first)
    def _():
        for copy in down:
            copy.start()

    @pl.when(head == 0)
    def _():
        sides[0] = jnp.zeros((MAXLEN, width), bf16)

    @pl.when(head == n_head - 1)
    def _():
        sides[1] = jnp.zeros((MAXLEN, width), bf16)

    def stored(at, n):
        return pltpu.make_async_copy(
            work.at[pl.ds(at, ROWS)], qkv_hbm.at[pl.ds(at, ROWS)], out_sems.at[n]
        )

    def project(rows, at, n):
        into = pl.ds(at, ROWS)
        query = (dot(rows, w[:, :width], NN) + small[7:8, :]) * HEAD_DIM**-0.5
        work[into, :width] = query.astype(bf16)
        work[into, width : 2 * width] = dot(rows, w[:, width : 2 * width], NN).astype(bf16)
        value = dot(rows, w[:, 2 * width :], NN) + small[8:9, :]
        work[into, 2 * width :] = value.astype(bf16)
        stored(at, n).start()

    load.wait()

    def own_rows(n, carry):
        at = pl.multiple_of(n * ROWS, ROWS)
        project(tok[pl.ds(at, ROWS), :], pl.multiple_of(MAXLEN + at, ROWS), n)
        return carry

    lax.fori_loop(0, own // ROWS, own_rows, 0)

    n_seqs = lens.shape[1]
    rows_of[...] = jnp.zeros_like(rows_of)
    rows_of[0:1, :n_seqs] = lens[...]
    rows_of[1:2, :n_seqs] = labels[...]
    i, j = iota((SIDE, SIDE), 0), iota((SIDE, SIDE), 1)
    length, label = rows_of[0:1, :].astype(f32), rows_of[1:2, :].astype(f32)
    to_col = lambda row, chosen: jnp.sum(jnp.where(chosen, row, 0.0), axis=1, keepdims=True)
    length_col, ends_col = to_col(length, i == j), to_col(length, j <= i)
    ends = jnp.sum(jnp.where(i <= j, length_col, 0.0), axis=0, keepdims=True)
    starts = ends - length
    group = float(own * n_head)
    n_rows = seqs_of.shape[0]
    row, lane = i[:n_rows], j[:n_rows]
    first_col = jnp.where(row < n_seqs, (ends_col - length_col)[:n_rows], -1.0)
    label_col = to_col(label, i == j)[:n_rows]
    seqs_of[...] = jnp.where(lane == 0, first_col, jnp.where(lane == 1, label_col, 0.0)).astype(jnp.int32)

    base = head * own - MAXLEN
    row, lane = i[:16], j[:16]
    blk = (base + row * QBLK).astype(f32)
    taken = lane < n_seqs
    low = jnp.max(jnp.where(taken & (starts <= blk), starts, -1.0), axis=1, keepdims=True)
    high = jnp.min(
        jnp.where(taken & (ends > blk + (QBLK - 1)), ends, group), axis=1, keepdims=True
    )
    at = row * QBLK
    is_own = (at >= MAXLEN) & (at < MAXLEN + own)
    low = jnp.broadcast_to(low.astype(jnp.int32), at.shape) - base
    high = jnp.broadcast_to(high.astype(jnp.int32), at.shape) - base
    low = jnp.where(is_own, low, jnp.maximum(low, MAXLEN))
    high = jnp.where(is_own, high, jnp.minimum(high, MAXLEN + own))
    low = (low >> 7) << 7
    valid = (blk >= 0.0) & (blk < group)
    steps = jnp.where(valid, jnp.maximum((high - low + KCHUNK - 1) >> (KCHUNK.bit_length() - 1), 0), 0)
    bounds[...] = jnp.where(lane == 0, low, jnp.where(lane == 1, steps, 0))

    lane = iota((QBLK, SIDE), 1)

    def masks(n, carry):
        at = pl.multiple_of(n * QBLK, QBLK)
        pos = (iota((QBLK, SIDE), 0) + (base + at)).astype(f32)
        inside = ((starts <= pos) & (pos < ends)).astype(f32)
        hot[pl.ds(at, QBLK), :] = inside.astype(bf16)
        mask[pl.ds(at, QBLK), :] = jnp.where(lane < n_seqs, (inside - 1.0) * BIG, 1.0).astype(bf16)
        return carry

    lax.fori_loop(0, window // QBLK, masks, 0)
    mask[pl.ds(window, PAD), :] = jnp.where(iota((PAD, SIDE), 1) < n_seqs, -BIG, 1.0).astype(bf16)

    for n in range(pieces):

        @pl.when(not_first)
        def _():
            up[n].wait_recv()

        @pl.when(not_last)
        def _():
            down[n].wait_recv()

        def side_rows(side, carry):
            at = pl.multiple_of(side * (MAXLEN + own) + n * ROWS, ROWS)
            project(sides[side, here(n), :], at, own // ROWS + 2 * n + side)
            return carry

        lax.fori_loop(0, 2, side_rows, 0)

    for n in range(own // ROWS):
        stored(MAXLEN + n * ROWS, n).wait()
    for n in range(pieces):
        for side in range(2):
            stored(side * (MAXLEN + own) + n * ROWS, own // ROWS + 2 * n + side).wait()

    @pl.when(not_last)
    def _():
        for copy in up:
            copy.wait_send()

    @pl.when(not_first)
    def _():
        for copy in down:
            copy.wait_send()


def front(tok, w_qkv, small, lens, labels):
    own, width = tok.shape
    window = own + 2 * MAXLEN
    seqs = lens.shape[1] + -lens.shape[1] % 16
    pieces = MAXLEN // ROWS
    shape = jax.ShapeDtypeStruct
    vmem, hbm = pl.BlockSpec(memory_space=pltpu.VMEM), pl.BlockSpec(memory_space=pl.ANY)
    return pl.pallas_call(
        front_kernel,
        in_specs=[vmem, hbm, vmem, vmem, vmem],
        out_specs=[hbm] + [vmem] * 4,
        out_shape=[
            shape((window, 3 * width), bf16),
            shape((window, SIDE), bf16),
            shape((window + PAD, SIDE), bf16),
            shape((16, SIDE), jnp.int32),
            shape((seqs, SIDE), jnp.int32),
        ],
        scratch_shapes=[
            pltpu.VMEM((2, MAXLEN, width), bf16),
            pltpu.VMEM(w_qkv.shape, bf16),
            pltpu.VMEM((window, 3 * width), bf16),
            pltpu.VMEM((8, SIDE), jnp.int32),
            pltpu.SemaphoreType.DMA,
            pltpu.SemaphoreType.DMA((own // ROWS + 2 * pieces,)),
            pltpu.SemaphoreType.DMA((2, pieces)),
            pltpu.SemaphoreType.DMA((2, pieces)),
        ],
        compiler_params=pltpu.CompilerParams(
            vmem_limit_bytes=40 * 2**20, collective_id=2, has_side_effects=True
        ),
        cost_estimate=pl.CostEstimate(
            flops=6 * window * width * width, bytes_accessed=16 * 2**20, transcendentals=0
        ),
        name="front",
    )(tok, w_qkv, small, lens, labels)


def grads_kernel(
    act_hbm, gpre_hbm, gs, gffn, mid, ctx, gattn, cls, gpool, tok,
    gsw, tok_t, *refs,
):
    outs, refs = refs[:7], refs[7:]
    outs = (*outs[:6], outs[6].at[0], outs[6].at[1])
    (act, gpre, mid_t, keep_a, send_a, got_a, keep_b, send_b, got_b, keep_c, send_c, got_c, split,
     loads, send_sems, recv_sems, halo_sems) = refs
    seq, head = lax.axis_index("seq"), lax.axis_index("head")
    n_head = lax.axis_size("head")
    core = lax.rem(seq, 2)
    chunks, own, width = act.shape
    half_b, half_w = keep_a.shape[1], keep_b.shape[2]
    for c in range(chunks):
        pltpu.make_async_copy(act_hbm.at[c], act.at[c], loads.at[c]).start()
        pltpu.make_async_copy(gpre_hbm.at[c], gpre.at[c], loads.at[chunks + c]).start()

    barrier = pltpu.get_barrier_semaphore()
    pl.semaphore_signal(barrier, inc=1, device_id={"seq": seq ^ OTHER_CORE}, device_id_type=MESH)

    @pl.when(head > 0)
    def _():
        pl.semaphore_signal(barrier, inc=1, device_id={"head": head - 1}, device_id_type=MESH)

    @pl.when(head < n_head - 1)
    def _():
        pl.semaphore_signal(barrier, inc=1, device_id={"head": head + 1}, device_id_type=MESH)

    pl.semaphore_wait(barrier, 1 + (head > 0).astype(jnp.int32) + (head < n_head - 1).astype(jnp.int32))

    up = pltpu.make_async_remote_copy(
        src_ref=gs.at[pl.ds(own - MAXLEN, MAXLEN)], dst_ref=gsw.at[pl.ds(0, MAXLEN)],
        send_sem=halo_sems.at[0], recv_sem=halo_sems.at[1],
        device_id={"head": lax.rem(head + 1, n_head)}, device_id_type=MESH,
    )
    down = pltpu.make_async_remote_copy(
        src_ref=gs.at[pl.ds(0, MAXLEN)], dst_ref=gsw.at[pl.ds(own + MAXLEN, MAXLEN)],
        send_sem=halo_sems.at[2], recv_sem=halo_sems.at[3],
        device_id={"head": lax.rem(head + n_head - 1, n_head)}, device_id_type=MESH,
    )
    stay = pltpu.make_async_copy(gs, gsw.at[pl.ds(MAXLEN, own)], halo_sems.at[4])

    @pl.when(head < n_head - 1)
    def _():
        up.start()

    @pl.when(head > 0)
    def _():
        down.start()

    stay.start()

    def to_core(send, got, first, n):
        return pltpu.make_async_remote_copy(
            src_ref=send.at[n], dst_ref=got.at[n],
            send_sem=send_sems.at[first + n], recv_sem=recv_sems.at[first + n],
            device_id={"seq": seq ^ OTHER_CORE}, device_id_type=MESH,
        )

    copy_a = lambda n: to_core(send_a, got_a, 0, n)
    copy_b = lambda n: to_core(send_b, got_b, chunks, n)
    copy_c = lambda n: to_core(send_c, got_c, 2 * chunks, n)

    def put(tile, half, keep, send):
        mine, theirs = halves(tile, core, half)
        for g in range(len(mine)):
            keep[g] = mine[g]
            send[g] = theirs[g]

    mid_t[...] = mid[...].T
    put(dot(ctx[...], gattn[...], TN), half_w, keep_c.at[0], send_c.at[0])
    put(dot(cls[...], gpool[...], TN), half_w, keep_c.at[1], send_c.at[1])

    def chunk(c, carry):
        pltpu.make_async_copy(gpre_hbm.at[c], gpre.at[c], loads.at[chunks + c]).wait()
        put(dot(mid_t[...], gpre[c], NN), half_w, keep_b.at[c], send_b.at[c])

        @pl.when(c == 0)
        def _():
            copy_c(0).start()
            copy_c(1).start()

        @pl.when(c > 0)
        def _():
            copy_a(jnp.maximum(c - 1, 0)).start()

        pltpu.make_async_copy(act_hbm.at[c], act.at[c], loads.at[c]).wait()
        mine, theirs = halves(dot(act[c], gffn[...], TN), core, half_b)
        keep_a[c], send_a[c] = mine[0], theirs[0]
        copy_b(c).start()
        return carry

    lax.fori_loop(0, chunks, chunk, 0)

    tok_t[...] = tok[...].T

    place = seq // 2
    quarter = half_w // 4
    rows_a = half_b // 4
    turns = (1, 2, 3, 0)
    for n in range(2):
        copy_c(n).wait_recv()
        for r in turns:
            total = keep_c[n, place ^ r].astype(f32) + got_c[n, place ^ r].astype(f32)
            for h in range(4):
                outs[r][h, rows_a + n * quarter : rows_a + (n + 1) * quarter, :] = total[
                    h * quarter : (h + 1) * quarter
                ].astype(outs[r].dtype)
    copy_a(chunks - 1).start()

    def sum_b(c, carry):
        copy_b(c).wait_recv()
        for g in range(4):
            total = keep_b[c, g].astype(f32) + got_b[c, g].astype(f32)
            for h in range(4):
                split[h, g] = total[h * quarter : (h + 1) * quarter]
        cols = pl.ds(pl.multiple_of(c * width, width), width)
        for r in range(4):
            for g in range(4):
                outs[4 + r][g, :, cols] = split[head ^ r, g].astype(outs[4 + r].dtype)
        return carry

    lax.fori_loop(0, chunks, sum_b, 0)
    for c in range(chunks):
        copy_a(c).wait_recv()
    for r in turns:
        total = keep_a[place ^ r].astype(f32) + got_a[place ^ r].astype(f32)
        for h in range(4):
            outs[r][h, :rows_a, :] = total[h * rows_a : (h + 1) * rows_a].astype(outs[r].dtype)
    for c in range(chunks):
        copy_a(c).wait_send()
        copy_b(c).wait_send()
    for n in range(2):
        copy_c(n).wait_send()
    stay.wait()

    @pl.when(head < n_head - 1)
    def _():
        up.wait_send()
        down.wait_recv()

    @pl.when(head > 0)
    def _():
        up.wait_recv()
        down.wait_send()


def send_grads(act, gpre, gs, gffn, mid, ctx, gattn, cls, gpool, tok):
    chunks, own, width = act.shape
    half_b, half_w = chunks * width // 8, width // 8
    window = own + 2 * MAXLEN
    shape = jax.ShapeDtypeStruct
    vmem, hbm = pl.BlockSpec(memory_space=pltpu.VMEM), pl.BlockSpec(memory_space=pl.ANY)
    kinds = (f32, bf16, bf16, bf16)
    return pl.pallas_call(
        grads_kernel,
        in_specs=[hbm, hbm] + [vmem] * 8,
        out_specs=[hbm] + [vmem] * 8,
        out_shape=[shape((window, width + SIDE), bf16), shape((width, own), bf16)]
        + [shape((4, half_b // 4 + half_w // 2, width), k) for k in kinds]
        + [shape((4, half_w // 4, chunks * width), k) for k in kinds[:2]]
        + [shape((2, 4, half_w // 4, chunks * width), bf16)],
        scratch_shapes=[
            pltpu.VMEM((chunks, own, width), bf16),
            pltpu.VMEM((chunks, own, width), bf16),
            pltpu.VMEM((width, own), bf16),
        ]
        + [pltpu.VMEM((chunks, half_b, width), bf16)] * 3
        + [pltpu.VMEM((chunks, 4, half_w, width), bf16)] * 3
        + [pltpu.VMEM((2, 4, half_w, width), bf16)] * 3
        + [
            pltpu.VMEM((4, 4, half_w // 4, width), f32),
            pltpu.SemaphoreType.DMA((2 * chunks,)),
            pltpu.SemaphoreType.DMA((2 * chunks + 2,)),
            pltpu.SemaphoreType.DMA((2 * chunks + 2,)),
            pltpu.SemaphoreType.DMA((5,)),
        ],
        compiler_params=pltpu.CompilerParams(
            vmem_limit_bytes=60 * 2**20, collective_id=0, has_side_effects=True
        ),
        cost_estimate=pl.CostEstimate(
            flops=2 * own * width * width * (2 * chunks + 1), bytes_accessed=30 * 2**20, transcendentals=0
        ),
        name="send_grads",
    )(act, gpre, gs, gffn, mid, ctx, gattn, cls, gpool, tok)


def finish_kernel(n_parts, *refs):
    inputs, refs = refs[: 10 + 4 * n_parts], refs[10 + 4 * n_parts :]
    sends_q = inputs[9 : 9 + n_parts]
    gtok, sum_a, sum_b, sum_out, sum_pool, sum_q, sum_v = refs[:7]
    n_held = 8 + 3 * n_parts
    held, refs = refs[7 : 7 + n_held], refs[7 + n_held :]
    own_a, near_a, own_b, near_b, vec = held[0], held[1:4], held[4], (held[5], held[6].at[0]), held[7]
    keeps, vec_parts, parts = (held[8 + n * n_parts : 8 + (n + 1) * n_parts] for n in range(3))
    (w_qkv, all_a, send_a, got_a, all_b, send_b, got_b, got_f, got_q, own_q, send_n, got_n, all_q, send_z, got_z,
     vecs, got_v, loads, send_sems, recv_sems) = refs
    wanted = inputs[:8] + inputs[9 + n_parts : -1] + (inputs[8], inputs[-1])
    copies = [
        pltpu.make_async_copy(src, dst, loads.at[n])
        for n, (src, dst) in enumerate(zip(wanted, held + (w_qkv, gtok)))
    ]
    for copy in copies:
        copy.start()
    seq, head = lax.axis_index("seq"), lax.axis_index("head")
    place = seq // 2
    width = gtok.shape[1]
    quarter = width // 32
    cols = width // n_parts
    line = (1, 2, 3)
    greet(
        [{"seq": seq ^ OTHER_CORE}]
        + [{"seq": seq ^ near} for near in NEAR]
        + [{"head": head ^ r} for r in line]
    )
    sends = Sends(send_sems, recv_sems)
    for r in line:
        sends.plan(("a", r), send_a.at[r - 1], got_a.at[r - 1], head=head ^ r)
        sends.plan(("b", r), send_b.at[r - 1], got_b.at[r - 1], seq=seq ^ NEAR[r - 1])
    for p in range(n_parts):
        sends.plan(("core", p), sends_q[p], got_q.at[p], seq=seq ^ OTHER_CORE)
        for r in line:
            sends.plan(("near", p, r), send_n.at[p, r - 1], got_n.at[p, r - 1], seq=seq ^ NEAR[r - 1])
            sends.plan(("line", p, r), send_z.at[p, r - 1], got_z.at[p, r - 1], head=head ^ r)
    sends.plan(("core", "v"), vecs.at[0], got_v.at[0], seq=seq ^ OTHER_CORE)
    for r in line:
        sends.plan(("near", "v", r), vecs.at[1], got_v.at[r], seq=seq ^ NEAR[r - 1])
        sends.plan(("line", "v", r), vecs.at[2], got_v.at[3 + r], head=head ^ r)
    sends.plan("pass", inputs[6].at[1], got_f, head=head ^ 1)
    sends.start(*[("core", p) for p in range(n_parts)])
    sends.start("pass")

    for copy in copies[: 8 + 2 * n_parts]:
        copy.wait()
    rows_v = vec.shape[0]
    vecs[0, :rows_v, :] = vec[...]
    for p in range(n_parts):
        vecs[0, rows_v:, p * cols : (p + 1) * cols] = vec_parts[p][...]
    for h in range(4):
        all_a[h] = (own_a[h] + near_a[0][h].astype(f32)) + (
            near_a[1][h].astype(f32) + near_a[2][h].astype(f32)
        )
    for r in line:
        send_a[r - 1] = all_a[head ^ r].astype(bf16)
    sends.start(("core", "v"))

    def start_near(p):
        sends.start(*[("near", p, r) for r in line])

    for p in range(n_parts):
        sends.arrived(("core", p))
        for r in line:
            for n in range(3):
                send_n[p, r - 1, n] = (
                    keeps[p][n, place ^ r].astype(f32) + got_q[p, n, place ^ r].astype(f32)
                ).astype(bf16)
        for n in range(3):
            own_q[p, n] = keeps[p][n, place].astype(f32) + got_q[p, n, place].astype(f32)
        if p == 0:
            sends.start(*[("a", r) for r in line])
        else:
            start_near(p - 1)
    start_near(n_parts - 1)
    sends.arrived(("core", "v"))
    vecs[1] = vecs[0] + got_v[0]
    sends.arrived("pass")
    for g in range(4):
        all_b[g] = (own_b[g] + near_b[0][g].astype(f32)) + (
            near_b[1][g].astype(f32) + got_f[g].astype(f32)
        )
    for r in line:
        send_b[r - 1] = all_b[place ^ r].astype(bf16)
    for copy in copies[8 + 2 * n_parts :]:
        copy.wait()

    def back(n, carry):
        here = pl.ds(pl.multiple_of(n * width, width), width)
        gtok[...] += dot(jnp.concatenate([p[n] for p in parts], axis=1), w_qkv[:, here], NT)

        @pl.when(n == 0)
        def _():
            sends.start(*[("near", "v", r) for r in line])
            sends.start(*[("b", r) for r in line])

        return carry

    lax.fori_loop(0, 3, back, 0)

    for p in range(n_parts):
        sends.arrived(*[("near", p, r) for r in line])
        for h in range(4):
            rows = slice(h * quarter, (h + 1) * quarter)
            for n in range(3):
                all_q[p, h, n] = (own_q[p, n, rows, :] + got_n[p, 0, n, rows, :].astype(f32)) + (
                    got_n[p, 1, n, rows, :].astype(f32) + got_n[p, 2, n, rows, :].astype(f32)
                )
        for r in line:
            send_z[p, r - 1] = all_q[p, head ^ r].astype(bf16)
        if p > 0:
            sends.start(*[("line", p - 1, r) for r in line])
    sends.arrived(*[("near", "v", r) for r in line])
    vecs[2] = (vecs[1] + got_v[1]) + (got_v[2] + got_v[3])
    sends.start(*[("line", n_parts - 1, r) for r in line])
    sends.arrived(*[("a", r) for r in line])
    total = (all_a[head] + got_a[0].astype(f32)) + (got_a[1].astype(f32) + got_a[2].astype(f32))
    rows_a = sum_a.shape[0]
    sum_a[...] = total[:rows_a]
    sum_out[...] = total[rows_a : rows_a + quarter]
    sum_pool[...] = total[rows_a + quarter :]
    sends.start(*[("line", "v", r) for r in line])
    sends.arrived(*[("b", r) for r in line])
    sum_b[...] = (all_b[place] + got_b[0].astype(f32)) + (got_b[1].astype(f32) + got_b[2].astype(f32))
    for p in range(n_parts):
        sends.arrived(*[("line", p, r) for r in line])
        for n in range(3):
            at = n * width + p * cols
            sum_q[:, at : at + cols] = (all_q[p, head, n] + got_z[p, 0, n].astype(f32)) + (
                got_z[p, 1, n].astype(f32) + got_z[p, 2, n].astype(f32)
            )
    sends.arrived(*[("line", "v", r) for r in line])
    sum_v[...] = (vecs[2] + got_v[4]) + (got_v[5] + got_v[6])
    sends.drain()


def finish(gar, w_qkv, vec, parts, a, b):
    own, width = gar.shape
    half_w = width // 8
    quarter = half_w // 4
    n_parts = len(parts)
    cols = width // n_parts
    rows_z, ff = a[0].shape[1], b[0].shape[2]
    n_vec = vec.shape[0] + 8
    shape = jax.ShapeDtypeStruct
    vmem, hbm = pl.BlockSpec(memory_space=pltpu.VMEM), pl.BlockSpec(memory_space=pl.ANY)
    n_copies = 6 + 7 * n_parts + 7 + 1
    grads, keeps, sends, sums = ([p[n] for p in parts] for n in range(4))
    held = [*a, *b, vec, *keeps, *sums, *grads]
    return pl.pallas_call(
        functools.partial(finish_kernel, n_parts),
        in_specs=[hbm] * (10 + 4 * n_parts),
        out_specs=[vmem] * 7,
        out_shape=[
            shape((own, width), f32),
            shape((rows_z - 2 * quarter, width), f32),
            shape((quarter, ff), f32),
            shape((quarter, width), f32),
            shape((quarter, width), f32),
            shape((quarter, 3 * width), f32),
            shape((n_vec, width), f32),
        ],
        scratch_shapes=[pltpu.VMEM(h.shape, h.dtype) for h in held]
        + [
            pltpu.VMEM(w_qkv.shape, bf16),
            pltpu.VMEM((4, rows_z, width), f32),
            pltpu.VMEM((3, rows_z, width), bf16),
            pltpu.VMEM((3, rows_z, width), bf16),
            pltpu.VMEM((4, quarter, ff), f32),
            pltpu.VMEM((3, quarter, ff), bf16),
            pltpu.VMEM((3, quarter, ff), bf16),
            pltpu.VMEM((4, quarter, ff), bf16),
            pltpu.VMEM((n_parts, 3, 4, half_w, cols), bf16),
            pltpu.VMEM((n_parts, 3, half_w, cols), f32),
            pltpu.VMEM((n_parts, 3, 3, half_w, cols), bf16),
            pltpu.VMEM((n_parts, 3, 3, half_w, cols), bf16),
            pltpu.VMEM((n_parts, 4, 3, quarter, cols), f32),
            pltpu.VMEM((n_parts, 3, 3, quarter, cols), bf16),
            pltpu.VMEM((n_parts, 3, 3, quarter, cols), bf16),
            pltpu.VMEM((3, n_vec, width), f32),
            pltpu.VMEM((7, n_vec, width), f32),
            pltpu.SemaphoreType.DMA((len(held) + 2,)),
            pltpu.SemaphoreType.DMA((n_copies,)),
            pltpu.SemaphoreType.DMA((n_copies,)),
        ],
        compiler_params=pltpu.CompilerParams(
            vmem_limit_bytes=56 * 2**20, collective_id=1, has_side_effects=True
        ),
        cost_estimate=pl.CostEstimate(
            flops=12 * own * width * width, bytes_accessed=12 * 2**20, transcendentals=0
        ),
        name="finish",
    )(*a, *b, vec, w_qkv, *sends, *keeps, *sums, *grads, gar)


def halo(rows, left_axis, n_head):
    up = [(i, i + 1) for i in range(n_head - 1)]
    down = [(i + 1, i) for i in range(n_head - 1)]
    from_left = lax.ppermute(rows[-MAXLEN:], left_axis, up)
    from_right = lax.ppermute(rows[:MAXLEN], left_axis, down)
    return jnp.concatenate([from_left, rows, from_right], axis=0)


def pick(values, axis, index):
    return lax.dynamic_index_in_dim(values, index, axis, keepdims=False)


class Sums:
    def __init__(self, pairs, orders, n_seq, n_head, vectors):
        self.count = {"seq": n_seq, "head": n_head}
        self.bits = {"seq": n_seq.bit_length() - 1, "head": n_head.bit_length() - 1}
        self.stages = sum(self.bits.values())
        self.orders = orders
        self.vectors = vectors
        self.axes = [[n for n in range(self.stages) if n != self.bits["seq"] - 1] for _ in pairs]
        shape = lambda a: a.reshape(
            (2,) * (self.stages - 1) + (a.shape[1] // n_head,) + a.shape[2:]
        )
        self.kept = [shape(keep) for keep, _ in pairs]
        self.sent = [shape(send) for _, send in pairs]
        self.stage = 0
        self.send()

    def send(self):
        self.got = [
            self.swap(v, *self.orders[n][self.stage]) for n, v in enumerate(self.sent)
        ]
        self.vectors = self.vectors + self.swap(self.vectors, *self.orders[0][self.stage])

    def swap(self, values, name, bit):
        return lax.ppermute(values, name, [(i, i ^ (1 << bit)) for i in range(self.count[name])])

    def split(self):
        self.stage += 1
        kept, sent = [], []
        for n, (keep, got) in enumerate(zip(self.kept, self.got)):
            name, bit = self.orders[n][self.stage]
            where = (self.stages if name == "head" else self.bits["seq"]) - 1 - bit
            at = self.axes[n].index(where)
            self.axes[n].pop(at)
            mine = (lax.axis_index(name) >> bit) & 1
            half = lambda m: pick(keep, at, m).astype(f32) + pick(got, at, m).astype(f32)
            sent.append(half(1 - mine).astype(bf16))
            kept.append(half(mine))
        self.kept, self.sent = kept, sent

    def rest(self):
        while self.stage < self.stages - 1:
            self.split()
            self.send()
        return [k.astype(f32) + g.astype(f32) for k, g in zip(self.kept, self.got)]


def after(value, *others):
    return lax.optimization_barrier((value, *others))[0]


def orders(n_seq, n_head):
    seq_bits, head_bits = n_seq.bit_length() - 1, n_head.bit_length() - 1
    core = [("seq", 0)]
    planar = [("seq", b) for b in range(1, seq_bits)]
    along = [("head", b) for b in range(head_bits)]
    return (
        core + planar + along,
        core + planar[::-1] + along,
        core + along + planar,
    )


def local(
    tokens, cotangent, lengths, labels, w_qkv, b_query, b_value, w_out, b_out, gain_attn,
    shift_attn, w_in, b_in, w_back, b_back, gain_ffn, shift_ffn, w_pool, b_pool, w_class,
):
    n_head = lax.axis_size("head")
    n_seq = lax.axis_size("seq")
    head_index = lax.axis_index("head")
    own, width = tokens.shape
    window = own + 2 * MAXLEN
    group = own * n_head

    small = jnp.stack(
        [b_out, gain_attn, shift_attn, b_back, gain_ffn, shift_ffn, b_pool, b_query, b_value]
    )
    if (n_seq, n_head) == (8, 4):
        qkv, hot, mask, bounds, seqs_of = front(tokens, w_qkv, small, lengths, labels)
    else:
        seq_lengths = lengths[0]
        ends = jnp.cumsum(seq_lengths)
        starts = ends - seq_lengths
        base = head_index * own - MAXLEN
        pos = base + jnp.arange(window, dtype=jnp.int32)
        n_in_group = seq_lengths.shape[0]
        lane_pad = (0, SIDE - n_in_group)
        starts_w = jnp.pad(starts, lane_pad, constant_values=group + MAXLEN)
        ends_w = jnp.pad(ends, lane_pad, constant_values=-MAXLEN)
        inside = (starts_w[None, :] <= pos[:, None]) & (pos[:, None] < ends_w[None, :])
        hot = inside.astype(bf16)
        lane = jnp.arange(SIDE, dtype=jnp.int32)[None, :]
        mask = jnp.where(lane < n_in_group, jnp.where(inside, 0.0, -BIG), 1.0).astype(bf16)
        mask = jnp.concatenate(
            [mask, jnp.broadcast_to(jnp.where(lane < n_in_group, -BIG, 1.0).astype(bf16), (PAD, SIDE))]
        )
        blk = base + QBLK * jnp.arange(window // QBLK, dtype=jnp.int32)
        low = jnp.max(jnp.where(starts[None, :] <= blk[:, None], starts[None, :], -1), axis=1)
        high = jnp.min(
            jnp.where(ends[None, :] > blk[:, None] + QBLK - 1, ends[None, :], group), axis=1
        )
        is_own = (blk >= base + MAXLEN) & (blk < base + MAXLEN + own)
        low = jnp.where(is_own, low - base, jnp.maximum(low - base, MAXLEN))
        high = jnp.where(is_own, high - base, jnp.minimum(high - base, MAXLEN + own))
        valid = (blk >= 0) & (blk < group)
        low = low // 128 * 128
        steps = jnp.where(valid, jnp.maximum((high - low + KCHUNK - 1) // KCHUNK, 0), 0)
        bounds = jnp.stack([low, steps], axis=1).astype(jnp.int32)
        seq_pad = (0, -n_in_group % 16)
        seqs_of = jnp.stack(
            [jnp.pad(starts, seq_pad, constant_values=-1), jnp.pad(labels[0], seq_pad)], axis=1
        )
        tokens_w = halo(tokens, "head", n_head)
        bias = jnp.concatenate([b_query, jnp.zeros_like(b_query), b_value])[None, :]
        qscale = jnp.where(jnp.arange(3 * width) < width, HEAD_DIM**-0.5, 1.0).astype(f32)[None, :]
        qkv = ((dot(tokens_w, w_qkv, NN) + bias) * qscale).astype(bf16)
    context, lse = attend(bounds, qkv, hot, mask, own)

    shards = n_seq * n_head
    shard = head_index + n_head * lax.axis_index("seq")
    core = (lax.axis_index("seq") & 1).reshape(1)
    (output, gar, gs, act, gpre, gffn, mid, gattn, cls, gpool, vec) = middle_layer(
        2 * fold_of(width // PAIR, 3), head_index.reshape(1), w_in, w_back, w_pool, tokens, context, lse,
        cotangent, w_out, b_in.reshape(1, -1), w_class.T, small, seqs_of,
    )
    pairs = width // PAIR
    fold = fold_of(pairs, 2)
    parts = pairs // fold
    gqkv = []
    if (n_seq, n_head) == (8, 4):
        grads_w, tok_t, *pieces = send_grads(act, gpre, gs, gffn, mid, context, gattn, cls, gpool, tokens)
        to = lambda v, axis, count, x: lax.ppermute(v, axis, [(i, i ^ x) for i in range(count)])
        a = [pieces[0]] + [to(pieces[r], "seq", 8, NEAR[r - 1]) for r in (1, 2, 3)]
        b = [pieces[4], to(pieces[5], "head", 4, 1), to(pieces[6], "head", 4, 2)]
        for part in range(parts):
            gqkv.append(attend_back(part, fold, bounds, qkv, grads_w, hot, mask, own, (tok_t, core)))
        grad_tokens, sum_wback, sum_win, sum_wout, sum_pool, sum_wqkv, summed = finish(
            gar, w_qkv, vec, gqkv, a, b
        )
        vectors, vectors_qkv = summed[: vec.shape[0]], summed[vec.shape[0] :]
    else:
        grads_w = halo(gs, "head", n_head)

        pieces = weight_grads(core, n_seq, act, gpre, gffn, mid, context, gattn, cls, gpool)
        orders_all = orders(n_seq, n_head)
        first = Sums(
            [pieces[0:2], pieces[2:4], pieces[4:6]], orders_all, n_seq, n_head, vec
        )
        for part in range(parts):
            gqkv.append(attend_back(part, fold, bounds, qkv, grads_w, hot, mask, own))
            bounds = after(bounds, gqkv[-1][0, :8, :128])
            if part + 1 < parts:
                first.split()
                sums = lax.optimization_barrier(tuple(first.sent) + (bounds, first.vectors))
                first.sent, bounds, first.vectors = list(sums[:3]), sums[3], sums[4]
                first.send()
        last_out = last_layer(core, n_seq, tokens, gar, w_qkv, gqkv)
        grad_tokens, vec_qkv = last_out[:2]
        last = Sums(
            [last_out[2:4], last_out[4:6], last_out[6:8]], orders_all, n_seq, n_head, vec_qkv
        )
        sum_wback, sum_win, sum_c = first.rest()
        sum_wout, sum_pool = sum_c[:, :width], sum_c[:, width:]
        sum_q, sum_k, sum_v = last.rest()
        sum_wqkv = jnp.concatenate([sum_q, sum_k, sum_v], axis=1)

        vectors, vectors_qkv = first.vectors, last.vectors
    size = width // shards
    mine = lax.dynamic_slice_in_dim(vectors, shard * size, size, 1)
    mine_qkv = lax.dynamic_slice_in_dim(vectors_qkv, shard * size, size, 1)
    chunks = w_in.shape[1] // width
    n_class = w_class.shape[1]
    grad_bin = lax.dynamic_slice_in_dim(
        vectors[8 : 8 + chunks].reshape(-1), shard * size * chunks, size * chunks, 0
    )
    grad_class = mine[8 + chunks : 8 + chunks + n_class].T
    entropy_mean = vectors[7, 0] / (n_seq * labels.shape[1])
    return (
        output, grad_tokens, sum_wqkv, mine_qkv[0], mine_qkv[2], sum_wout, mine[0], mine[1], mine[2],
        sum_win, grad_bin, sum_wback, mine[3], mine[4], mine[5], sum_pool, mine[6], grad_class,
        entropy_mean,
    )


def solution(mesh):
    rows = P(("seq", "head"), None)
    vec = P(("seq", "head"))
    return jax.shard_map(
        local,
        mesh=mesh,
        in_specs=(rows, rows, P("seq", None), P("seq", None)) + (P(),) * 16,
        out_specs=(
            rows, rows, rows, vec, vec, rows, vec, vec, vec, rows, vec, rows, vec, vec, vec, rows,
            vec, rows, P(),
        ),
        check_vma=False,
    )
```

profile of v0, /device:TPU:0, one launch (start us, length us, event | category | flops | bytes accessed | tf_op | source)
XLA Modules:
  0.0 269.9 jit_solution(6821707652187434309)
XLA Ops:
  0.7 0.7 stack.30
  1.3 0.7 stack.31
  2.0 0.7 stack.32
  2.7 0.7 stack.33
  3.4 0.7 stack.34
  4.1 0.7 stack.35
  4.8 0.7 stack.36
  5.5 0.7 stack.37
  6.2 0.7 stack.38
  6.9 2.0 copy-done.3
  8.9 1.3 copy-done.6
  10.2 0.7 copy-done.7
  10.9 0.7 copy-done.8
  11.5 25.1 %front.1 = (bf16[1792,2304]{1,0:T(8,128)(2,1)S(1)}, bf16[1792,128]{1,0:T(8,128)(2,1)S(1)}, bf16[1920,128]{1,0:T(8,128)(2,1)S(1)}, s32[16,128]{1,0:T(8,128)S(1)}, s32[32,128]{1,0:T(8,128)S(1)}) custom-call(bf16[768,768]{1,0:T(8,128)(2,1)S(1)} %copy-done.6, bf16[768,2304]{1,0:T(8,128)(2,1)S(1)} %copy-done.3, f32[9,768]{1,0:T(8,128)S(1)} %stack.39.small, ...), custom_call_target="tpu_custom_call" | custom-call | flops 6341787648 | bytes 16777216 | tf_op jit(solution)/shard_map/front/pallas_call | solution.py:864
  36.7 3.2 %copy-done = bf16[1792,2304]{1,0:T(8,128)(2,1)} copy-done((bf16[1792,2304]{1,0:T(8,128)(2,1)}, bf16[1792,2304]{1,0:T(8,128)(2,1)S(1)}, u32[]{:S(2)}) %copy-start) | copy-done | bytes 8257560
  39.9 0.8 copy-done.1
  40.7 0.8 copy-done.2
  41.4 0.6 copy-done.4
  42.0 0.6 copy-done.9
  42.6 22.2 %attend.1 = (bf16[768,768]{1,0:T(8,128)(2,1)}, f32[16,768]{1,0:T(8,128)}) custom-call(s32[16,128]{1,0:T(8,128)} %copy-done.4, bf16[1792,2304]{1,0:T(8,128)(2,1)} %copy-done, bf16[1792,2304]{1,0:T(8,128)(2,1)} %copy-done, bf16[1792,2304]{1,0:T(8,128)(2,1)} %copy-done, bf16[1792,128]{1,0:T(8,128)(2,1)} %copy-done.2, bf16[1920,128]{1,0:T(8,128)(2,1)} %copy-done.1), custom_call_target="tpu_custom_call" | custom-call | flops 1415577600 | bytes 8257536 | tf_op jit(solution)/shard_map/attend/pallas_call | solution.py:118
  64.8 38.0 %middle_layer.1 = (bf16[768,768]{1,0:T(8,128)(2,1)}, f32[768,768]{1,0:T(8,128)}, bf16[768,896]{1,0:T(8,128)(2,1)}, bf16[4,768,768]{2,1,0:T(8,128)(2,1)}, bf16[4,...) custom-call(s32[1]{0:T(128)} %bitcast.place, ...), custom_call_target="tpu_custom_call" | custom-call | flops 19931332608 | bytes 31457280 | tf_op jit(solution)/shard_map/middle_layer/pallas_call | solution.py:503
  102.9 34.4 %send_grads.1 = (bf16[1792,896]{1,0:T(8,128)(2,1)}, bf16[768,768]{1,0:T(8,128)(2,1)}, f32[4,144,768]{2,1,0:T(8,128)}, bf16[4,144,768]{2,1,0:T(8,128)(2,1)}, bf16...) custom-call(bf16[4,768,768]{2,1,0:T(8,128)(2,1)} %get-tuple-element., ...), custom_call_target="tpu_custom_call" | custom-call | flops 8153726976 | bytes 31457280 | tf_op jit(solution)/shard_map/send_grads/pallas_call | solution.py:1049
  137.3 1.5 collective-permute-start.4
  138.8 1.5 collective-permute-start
  140.3 1.5 collective-permute-start.1
  141.8 1.2 collective-permute-start.2
  143.0 0.2 collective-permute-start.3
  143.2 17.1 %attend_back2.1 = (bf16[3,768,256]{2,1,0:T(8,128)(2,1)}, bf16[3,4,96,256]{3,2,1,0:T(8,128)(2,1)}, bf16[3,4,96,256]{3,2,1,0:T(8,128)(2,1)}, f32[8,256]{1,0:T(8,128)}) custom-call(s32[16,128]{1,0:T(8,128)} %copy-done.4, bf16[1792,2304]{1,0:T(8,128)(2,1)} %copy-done, bf16[1792,2304]{1,0:T(8,128)(2,1)} %copy-done, bf16[1792,2304]{1,0:T(8,128)(2,1)} %copy-done, ...), custom_call_target="tpu_custom_call" | custom-call | flops 2831155200 | bytes 3670016 | tf_op jit(solution)/shard_map/attend_back2/pallas_call | solution.py:260
  160.3 17.1 %attend_back1.1 = (bf16[3,768,256]{2,1,0:T(8,128)(2,1)}, bf16[3,4,96,256]{3,2,1,0:T(8,128)(2,1)}, bf16[3,4,96,256]{3,2,1,0:T(8,128)(2,1)}, f32[8,256]{1,0:T(8,128)}) custom-call(s32[16,128]{1,0:T(8,128)} %copy-done.4, bf16[1792,2304]{1,0:T(8,128)(2,1)} %copy-done, bf16[1792,2304]{1,0:T(8,128)(2,1)} %copy-done, bf16[1792,2304]{1,0:T(8,128)(2,1)} %copy-done, ...), custom_call_target="tpu_custom_call" | custom-call | flops 2831155200 | bytes 3670016 | tf_op jit(solution)/shard_map/attend_back1/pallas_call | solution.py:260
  177.4 17.3 %attend_back0.1 = (bf16[3,768,256]{2,1,0:T(8,128)(2,1)}, bf16[3,4,96,256]{3,2,1,0:T(8,128)(2,1)}, bf16[3,4,96,256]{3,2,1,0:T(8,128)(2,1)}, f32[8,256]{1,0:T(8,128)}) custom-call(s32[16,128]{1,0:T(8,128)} %copy-done.4, bf16[1792,2304]{1,0:T(8,128)(2,1)} %copy-done, bf16[1792,2304]{1,0:T(8,128)(2,1)} %copy-done, bf16[1792,2304]{1,0:T(8,128)(2,1)} %copy-done, ...), custom_call_target="tpu_custom_call" | custom-call | flops 2831155200 | bytes 3670016 | tf_op jit(solution)/shard_map/attend_back0/pallas_call | solution.py:260
  194.8 0.8 copy-done.13
  195.5 0.3 copy-done.11
  195.8 0.3 copy-done.12
  196.1 0.4 copy-done.10
  196.5 59.4 %finish.1 = (f32[768,768]{1,0:T(8,128)}, f32[96,768]{1,0:T(8,128)}, f32[24,3072]{1,0:T(8,128)}, f32[24,768]{1,0:T(8,128)}, f32[24,768]{1,0:T(8,128)}, /*index=5*/f32[24,2304]{1,0:T(8,128)}, f32[32,768]{1,0:T(8,128)}) custom-call(f32[4,144,768]{2,1,0:T(8,128)} %get-tuple-element.81.refs_0_, bf16[4,144,768]{2,1,0:T(8,128)(2,1)} %copy-done.11, ...), custom_call_target="tpu_custom_call" | custom-call | flops 5435817984 | bytes 12582912 | tf_op jit(solution)/shard_map/finish/pallas_call | solution.py:1232
  255.9 0.9 slice.47
  256.8 0.7 slice.44
  257.5 0.7 slice.51
  258.3 1.2 slice.57
  259.5 0.7 dynamic-slice_bitcast_fusion
  260.2 0.6 dynamic_slice.11
  261.4 0.6 dynamic-slice_bitcast_fusion.1
  262.1 3.3 %copy.45 = f32[768,768]{1,0:T(8,128)} copy(f32[768,768]{1,0:T(8,128)} %get-tuple-element.142) | data formatting | bytes 4718592
  265.4 0.7 copy.46
  266.1 0.6 copy.47
  266.7 0.7 copy.48
  267.4 0.7 copy.49
  268.1 0.6 copy.50
  (33 shorter events, 0.2 us)
Async XLA Ops:
  6.9 2.0 copy-start.3
  8.9 1.3 copy-start.6
  10.2 0.7 copy-start.7
  10.9 0.7 copy-start.8
  11.5 25.1 %copy-start.5 = (f32[9,768]{1,0:T(8,128)}, f32[9,768]{1,0:T(8,128)S(1)}, u32[]{:S(2)}) copy-start(f32[9,768]{1,0:T(8,128)S(1)} %stack.39.small) | copy-start | bytes 82948
  36.7 3.2 %copy-start = (bf16[1792,2304]{1,0:T(8,128)(2,1)}, bf16[1792,2304]{1,0:T(8,128)(2,1)S(1)}, u32[]{:S(2)}) copy-start(bf16[1792,2304]{1,0:T(8,128)(2,1)S(1)} %get-tuple-element.66.q_ref.k_ref.v_ref) | copy-start | bytes 24772612
  39.9 0.8 copy-start.1
  40.7 0.8 copy-start.2
  41.4 0.6 copy-start.4
  42.0 0.6 copy-start.9
  137.3 57.5 %collective-permute-start.4 = (bf16[2,4,24,3072]{3,2,1,0:T(8,128)(2,1)}, bf16[2,4,24,3072]{3,2,1,0:T(8,128)(2,1)S(1)}, u32[]{:S(2)}, u32[]{:S(2)}) collective-permute-start(bf16[2,4,24,3072]{3,2,1,0:T(8,128)(2,1)} %get-tuple-element.87), channel_id=1, source_target_pairs={{0,2},{1,3},{2,0},{3,1},{4,6},{5,7},{6,4},{7,5},{8,10},{9,11},{10,... | collective-permute-start | bytes 3538952 | tf_op jit(solution)/shard_map/ppermute | solution.py:1420
  138.8 55.9 %collective-permute-start = (bf16[4,144,768]{2,1,0:T(8,128)(2,1)}, bf16[4,144,768]{2,1,0:T(8,128)(2,1)S(1)}, u32[]{:S(2)}, u32[]{:S(2)}) collective-permute-start(bf16[4,144,768]{2,1,0:T(8,128)(2,1)} %get-tuple-element.82), channel_id=1, source_target_pairs={{0,8},{4,12},{8,0},{12,4},{16,24},{20,28},{24,16},{28,20},{1,9},{5... | collective-permute-start | bytes 2654216 | tf_op jit(solution)/shard_map/ppermute | solution.py:1420
  140.3 54.4 %collective-permute-start.1 = (bf16[4,144,768]{2,1,0:T(8,128)(2,1)}, bf16[4,144,768]{2,1,0:T(8,128)(2,1)S(1)}, u32[]{:S(2)}, u32[]{:S(2)}) collective-permute-start(bf16[4,144,768]{2,1,0:T(8,128)(2,1)} %get-tuple-element.83), channel_id=1, source_target_pairs={{0,16},{4,20},{8,24},{12,28},{16,0},{20,4},{24,8},{28,12},{1,17},{... | collective-permute-start | bytes 2654216 | tf_op jit(solution)/shard_map/ppermute | solution.py:1420
  141.8 52.9 %collective-permute-start.2 = (bf16[4,144,768]{2,1,0:T(8,128)(2,1)}, bf16[4,144,768]{2,1,0:T(8,128)(2,1)}, u32[]{:S(2)}, u32[]{:S(2)}) collective-permute-start(bf16[4,144,768]{2,1,0:T(8,128)(2,1)} %get-tuple-element.84), channel_id=1, source_target_pairs={{0,24},{4,28},{8,16},{12,20},{16,8},{20,12},{24,0},{28,4},{1,25},{... | collective-permute-start | bytes 2654216 | tf_op jit(solution)/shard_map/ppermute | solution.py:1420
  143.0 51.7 %collective-permute-start.3 = (bf16[4,24,3072]{2,1,0:T(8,128)(2,1)}, bf16[4,24,3072]{2,1,0:T(8,128)(2,1)S(1)}, u32[]{:S(2)}, u32[]{:S(2)}) collective-permute-start(bf16[4,24,3072]{2,1,0:T(8,128)(2,1)} %get-tuple-element.86), channel_id=1, source_target_pairs={{0,1},{1,0},{2,3},{3,2},{4,5},{5,4},{6,7},{7,6},{8,9},{9,8},{10,11... | collective-permute-start | bytes 1769480 | tf_op jit(solution)/shard_map/ppermute | solution.py:1420
  194.7 0.8 copy-start.13
  194.7 1.1 copy-start.11
  194.7 1.4 copy-start.12
  194.8 1.8 copy-start.10
  262.1 3.3 %copy-start.16 = (f32[24,2304]{1,0:T(8,128)S(1)}, f32[24,2304]{1,0:T(8,128)}, u32[]{:S(2)}) copy-start(f32[24,2304]{1,0:T(8,128)} %get-tuple-element.143) | copy-start | bytes 663556
  262.1 4.0 %copy-start.18 = (f32[24,768]{1,0:T(8,128)S(1)}, f32[24,768]{1,0:T(8,128)}, u32[]{:S(2)}) copy-start(f32[24,768]{1,0:T(8,128)} %get-tuple-element.146) | copy-start | bytes 221188
  262.1 4.6 %copy-start.15 = (f32[24,3072]{1,0:T(8,128)S(1)}, f32[24,3072]{1,0:T(8,128)}, u32[]{:S(2)}) copy-start(f32[24,3072]{1,0:T(8,128)} %get-tuple-element.150) | copy-start | bytes 884740
  265.4 2.0 copy-start.14
  265.4 2.8 %copy-start.17 = (f32[24,768]{1,0:T(8,128)S(1)}, f32[24,768]{1,0:T(8,128)}, u32[]{:S(2)}) copy-start(f32[24,768]{1,0:T(8,128)} %get-tuple-element.156) | copy-start | bytes 221188
where the time goes:
time: 273 us; the launch traced here: 270 us
  Pallas kernels  231 us (85%)
  local copies, waits for them, and re-layouts  30.8 us (11%)
  starting transfers between devices  5.95 us (2%)
    pallas_call x1, Pallas kernels, finish(): pl.pallas_call(functools.partial(finish_kernel, n_parts), in_specs=[hbm]...  59.4 us
    pallas_call x3, Pallas kernels, attend_back(): pl.pallas_call(functools.partial(attend_back_kernel, side0, len(extra)),...  51.5 us
    pallas_call x1, Pallas kernels, middle_layer(): pl.pallas_call(functools.partial(middle_kernel, heads_part), in_specs=[pl...  38 us
    pallas_call x1, Pallas kernels, send_grads(): pl.pallas_call(grads_kernel, in_specs=[hbm, hbm] + [vmem] * 8, out_specs=...  34.4 us
    pallas_call x1, Pallas kernels, front(): pl.pallas_call(front_kernel, in_specs=[vmem, hbm, vmem, vmem, vmem], out_...  25.1 us
    pallas_call x1, Pallas kernels, attend(): pl.pallas_call(attend_kernel, grid_spec=pltpu.PrefetchScalarGridSpec(num_...  22.2 us
    unnamed x44, local copies, waits for them, and re-layouts  19 us
    another operation x10, local copies, waits for them, and re-layouts, local(): jnp.stack([b_out, gain_attn, shift_attn, b_back, gain_ffn, shift_ffn, b_p...  6.27 us
  transfers between devices with their start and end apart: 5, of which 0 were waited for; matrix products, arithmetic and copies ran while one was open for 0% of the time, Pallas kernels for 19%

commit v1 on v0

--- a/solution.py
+++ b/solution.py
@@ -143,19 +143,25 @@
 
 def attend_back_kernel(side0, more, bounds, q_ref, k_ref, v_ref, do_ref, side_ref, hot_ref, mask_ref, *refs):
     extra, refs = refs[:more], refs[more:]
-    gqkv_ref, (kcat, vcat, kt, dk, dv) = refs[0], refs[-5:]
+    gqkv_ref, (kcat, vcat, kt, dk, dv) = refs[0].at[0], refs[-5:]
     window = k_ref.shape[0]
     own = gqkv_ref.shape[1]
     fold = kcat.shape[0]
-    low0, gap = side0
+    lanes, gap = side0
+    part = pl.program_id(0)
+    low0 = LSE0 + lanes * part
+
+    @pl.when(part == 0)
+    def _():
+        for j in range(fold):
+            kcat[j, :, PAIR:] = mask_ref[...]
+            vcat[j, :, PAIR:] = jnp.ones((window + PAD, SIDE), bf16)
+            kcat[j, pl.ds(window, PAD), :PAIR] = jnp.zeros((PAD, PAIR), bf16)
+            vcat[j, pl.ds(window, PAD), :PAIR] = jnp.zeros((PAD, PAIR), bf16)
+            kt[j, :, pl.ds(window, PAD)] = jnp.zeros((PAIR, PAD), bf16)
 
     for j in range(fold):
         cols = pl.ds(j * PAIR, PAIR)
-        kcat[j, :, PAIR:] = mask_ref[...]
-        vcat[j, :, PAIR:] = jnp.ones((window + PAD, SIDE), bf16)
-        kcat[j, pl.ds(window, PAD), :PAIR] = jnp.zeros((PAD, PAIR), bf16)
-        vcat[j, pl.ds(window, PAD), :PAIR] = jnp.zeros((PAD, PAIR), bf16)
-        kt[j, :, pl.ds(window, PAD)] = jnp.zeros((PAIR, PAD), bf16)
         kcat[j, pl.ds(0, window), :PAIR] = k_ref[:, cols]
         vcat[j, pl.ds(0, window), :PAIR] = v_ref[:, cols]
         for at in range(0, window, 256):
@@ -226,7 +232,7 @@
 
     if more:
         tok_t, place = extra[:2]
-        keep, send, sums = refs[1:4]
+        keep, send, sums = (ref.at[0] for ref in refs[1:4])
         sums[...] = jnp.zeros_like(sums)
 
         def third(n, carry):
@@ -241,32 +247,32 @@
         lax.fori_loop(0, 3, third, 0)
 
 
-def attend_back(part, fold, bounds, qkv, grads, hot, mask, own, extra=()):
+def attend_back(bounds, qkv, grads, hot, mask, own, extra=()):
     window, wide = qkv.shape
     width = wide // 3
     pairs = width // PAIR
+    fold = fold_of(pairs, 2)
     parts = pairs // fold
-    column = lambda c: pl.BlockSpec((window, fold * PAIR), lambda g, b: (0, c * parts + part))
+    cols = fold * PAIR
+    column = lambda c: pl.BlockSpec((window, cols), lambda g, b: (0, c * parts + g))
     whole = lambda a: pl.BlockSpec(a.shape, lambda g, b: (0, 0))
-    side0 = (LSE0 + 6 * fold * part, 6 * pairs)
     shape = jax.ShapeDtypeStruct
-    cols = fold * PAIR
     more_in, more_out = [], []
     if extra:
         more_in = [whole(extra[0]), pl.BlockSpec(memory_space=pltpu.SMEM)]
-        more_out = [shape((3, 4, width // 8, cols), bf16)] * 2 + [shape((8, cols), f32)]
-    block = lambda a: pl.BlockSpec(a.shape, lambda g, b: (0,) * len(a.shape))
-    outs = [shape((3, own, cols), bf16)] + more_out
+        more_out = [shape((parts, 3, 4, width // 8, cols), bf16)] * 2 + [shape((parts, 8, cols), f32)]
+    block = lambda a: pl.BlockSpec((1,) + a.shape[1:], lambda g, b: (g,) + (0,) * (len(a.shape) - 1))
+    outs = [shape((parts, 3, own, cols), bf16)] + more_out
     results = pl.pallas_call(
-        functools.partial(attend_back_kernel, side0, len(extra)),
+        functools.partial(attend_back_kernel, (6 * fold, 6 * pairs), len(extra)),
         grid_spec=pltpu.PrefetchScalarGridSpec(
             num_scalar_prefetch=1,
-            grid=(1,),
+            grid=(parts,),
             in_specs=[
                 column(0),
                 column(1),
                 column(2),
-                pl.BlockSpec((window, fold * PAIR), lambda g, b: (0, part)),
+                pl.BlockSpec((window, cols), lambda g, b: (0, g)),
                 pl.BlockSpec((window, SIDE), lambda g, b: (0, pairs)),
                 whole(hot),
                 whole(mask),
@@ -283,11 +289,9 @@
         ),
         out_shape=outs,
         cost_estimate=pl.CostEstimate(
-            flops=own * 900 * PAIR * fold * 16,
-            bytes_accessed=window * PAIR * fold * 8,
-            transcendentals=0,
+            flops=own * 900 * width * 16, bytes_accessed=window * width * 8, transcendentals=0
         ),
-        name=f"attend_back{part}",
+        name="attend_back",
     )(bounds, qkv, qkv, qkv, grads, grads, hot, mask, *extra)
     return results if extra else results[0]
 
@@ -326,12 +330,12 @@
 
 
 def middle_kernel(
-    heads_part, place, w_in_hbm, w_back_hbm, w_pool_hbm, tok, ctx, lse, cot, w_out, b_in, w_class, small, seqs_of,
-    out, gar, gs, act_hbm, gpre_hbm, gffn, mid, gattn, cls, gpool, vec,
-    w_in, w_back, w_pool, act, gpre, slope, unit_a, unit_f, inv_a, inv_f, acc, sems,
+    heads_part, place, w_in_hbm, w_back_hbm, w_pool_hbm, lse_hbm, cot_hbm, tok, ctx, w_out, b_in, w_class, small, seqs_of,
+    out_hbm, gar_hbm, gs_hbm, act_hbm, gpre_hbm, gffn_hbm, mid_hbm, gattn_hbm, cls, gpool, vec,
+    out, gar, gs, gffn, mid, gattn, lse, cot, more_sems, w_in, w_back, w_pool, act, gpre, slope, unit_a, unit_f, inv_a, inv_f, acc, sems,
 ):
     own, width = tok.shape
-    b_out, gain_a, shift_a, b_back, gain_f, shift_f, b_pool = (small[n : n + 1, :] for n in range(7))
+    b_out, gain_a, shift_a, b_back, gain_f, shift_f, b_pool = (small[:, n * width : (n + 1) * width] for n in range(7))
     starts, labels = seqs_of[:, 0:1], seqs_of[:, 1:2]
     chunks, _, wide = act.shape
     blocks = own // ROWS
@@ -340,7 +344,20 @@
         pltpu.make_async_copy(w_in_hbm, w_in, sems.at[0]),
         pltpu.make_async_copy(w_back_hbm, w_back, sems.at[1]),
         pltpu.make_async_copy(w_pool_hbm, w_pool, sems.at[2]),
+        pltpu.make_async_copy(cot_hbm, cot, more_sems.at[0]),
+        pltpu.make_async_copy(lse_hbm, lse, more_sems.at[1]),
     ]
+    store_mid, store_out, store_gffn = (
+        pltpu.make_async_copy(src, dst, more_sems.at[2 + n])
+        for n, (src, dst) in enumerate(((mid, mid_hbm), (out, out_hbm), (gffn, gffn_hbm)))
+    )
+
+    def last_stores(b):
+        return [
+            pltpu.make_async_copy(src.at[at(b)], dst.at[at(b)], more_sems.at[5 + 3 * b + n])
+            for n, (src, dst) in enumerate(((gar, gar_hbm), (gs, gs_hbm), (gattn, gattn_hbm)))
+        ]
+
     for load in loads:
         load.start()
 
@@ -365,6 +382,7 @@
         return carry
 
     lax.fori_loop(0, blocks, first_norm, 0)
+    store_mid.start()
     loads[0].wait()
     loads[1].wait()
     acc[...] = jnp.zeros_like(acc)
@@ -390,6 +408,9 @@
         return carry
 
     lax.fori_loop(0, blocks, second_norm, 0)
+    store_out.start()
+    loads[3].wait()
+    loads[4].wait()
 
     loads[2].wait()
     seqs = starts.shape[0]
@@ -429,6 +450,7 @@
 
     zero = jnp.zeros((1, width), f32)
     sums_f = lax.fori_loop(0, blocks, second_back, (zero, zero, zero))
+    store_gffn.start()
     acc[...] = jnp.zeros_like(acc)
 
     def backward(c, carry):
@@ -475,6 +497,8 @@
         lse_parts = low3(-lse[:, rows])
         side_lse = sum(dot(part, spread[p], TN) for p, part in enumerate(lse_parts))
         gs[rows, width:] = side + side_lse.astype(bf16)
+        for copy in last_stores(b):
+            copy.start()
         return carry[0] + g_gain, carry[1] + g_shift, carry[2] + col_sum(low.astype(f32))
 
     sums_a = lax.fori_loop(0, blocks, first_back, (zero, zero, zero))
@@ -489,6 +513,11 @@
     for c in range(chunks):
         pltpu.make_async_copy(act.at[c], act_hbm.at[c], sems.at[3 + c]).wait()
         pltpu.make_async_copy(gpre.at[c], gpre_hbm.at[c], sems.at[3 + chunks + c]).wait()
+    for copy in (store_mid, store_out, store_gffn):
+        copy.wait()
+    for b in range(blocks):
+        for copy in last_stores(b):
+            copy.wait()
 
 
 def middle_layer(heads_part, place, w_in, w_back, w_pool, tok, ctx, lse, cot, w_out, b_in, w_class, small, seqs_of):
@@ -502,8 +531,8 @@
     flops = 2 * own * width * (6 * width + 4 * ff)
     return pl.pallas_call(
         functools.partial(middle_kernel, heads_part),
-        in_specs=[pl.BlockSpec(memory_space=pltpu.SMEM), hbm, hbm, hbm] + [vmem] * 9,
-        out_specs=[vmem, vmem, vmem, hbm, hbm] + [vmem] * 6,
+        in_specs=[pl.BlockSpec(memory_space=pltpu.SMEM)] + [hbm] * 5 + [vmem] * 7,
+        out_specs=[hbm] * 8 + [vmem] * 3,
         out_shape=[
             shape((own, width), bf16),
             shape((own, width), f32),
@@ -518,6 +547,15 @@
             shape((VECTORS, width), f32),
         ],
         scratch_shapes=[
+            pltpu.VMEM((own, width), bf16),
+            pltpu.VMEM((own, width), f32),
+            pltpu.VMEM((own, width + SIDE), bf16),
+            pltpu.VMEM((own, width), bf16),
+            pltpu.VMEM((own, width), bf16),
+            pltpu.VMEM((own, width), bf16),
+            pltpu.VMEM(lse.shape, f32),
+            pltpu.VMEM(cot.shape, bf16),
+            pltpu.SemaphoreType.DMA((5 + 3 * (own // ROWS),)),
             pltpu.VMEM(w_in.shape, bf16),
             pltpu.VMEM(w_back.shape, bf16),
             pltpu.VMEM(w_pool.shape, bf16),
@@ -534,7 +572,7 @@
         compiler_params=pltpu.CompilerParams(vmem_limit_bytes=62 * 2**20),
         cost_estimate=pl.CostEstimate(flops=flops, bytes_accessed=30 * 2**20, transcendentals=0),
         name="middle_layer",
-    )(place, w_in, w_back, w_pool, tok, ctx, lse, cot, w_out, b_in, w_class, small, seqs_of)
+    )(place, w_in, w_back, w_pool, lse, cot, tok, ctx, w_out, b_in, w_class, small, seqs_of)
 
 
 def split_core(tile, core, half, keep, send, first):
@@ -755,10 +793,10 @@
 
     def project(rows, at, n):
         into = pl.ds(at, ROWS)
-        query = (dot(rows, w[:, :width], NN) + small[7:8, :]) * HEAD_DIM**-0.5
+        query = (dot(rows, w[:, :width], NN) + small[:, 7 * width : 8 * width]) * HEAD_DIM**-0.5
         work[into, :width] = query.astype(bf16)
         work[into, width : 2 * width] = dot(rows, w[:, width : 2 * width], NN).astype(bf16)
-        value = dot(rows, w[:, 2 * width :], NN) + small[8:9, :]
+        value = dot(rows, w[:, 2 * width :], NN) + small[:, 8 * width : 9 * width]
         work[into, 2 * width :] = value.astype(bf16)
         stored(at, n).start()
 
@@ -883,7 +921,7 @@
             pltpu.SemaphoreType.DMA((2, pieces)),
         ],
         compiler_params=pltpu.CompilerParams(
-            vmem_limit_bytes=40 * 2**20, collective_id=2, has_side_effects=True
+            vmem_limit_bytes=62 * 2**20, collective_id=2, has_side_effects=True
         ),
         cost_estimate=pl.CostEstimate(
             flops=6 * window * width * width, bytes_accessed=16 * 2**20, transcendentals=0
@@ -893,21 +931,38 @@
 
 
 def grads_kernel(
-    act_hbm, gpre_hbm, gs, gffn, mid, ctx, gattn, cls, gpool, tok,
-    gsw, tok_t, *refs,
+    ctx_hbm, gattn_hbm, mid_hbm, gffn_hbm, tok_hbm, gs_hbm, act_hbm, gpre_hbm, cls, gpool,
+    gsw, *refs,
 ):
-    outs, refs = refs[:7], refs[7:]
+    stores, outs, held, refs = refs[:8], refs[8:16], refs[16:22], refs[22:]
+    tok_t, (ctx, gattn, mid, gffn, tok, gs) = outs[7], held
+    store = [
+        pltpu.make_async_copy(src, dst, refs[-1].at[6 + n])
+        for n, (src, dst) in enumerate(zip(outs, stores))
+    ]
+    load = [
+        pltpu.make_async_copy(src, dst, refs[-1].at[n])
+        for n, (src, dst) in enumerate(
+            zip((ctx_hbm, gattn_hbm, mid_hbm, gffn_hbm, tok_hbm, gs_hbm), held)
+        )
+    ]
     outs = (*outs[:6], outs[6].at[0], outs[6].at[1])
     (act, gpre, mid_t, keep_a, send_a, got_a, keep_b, send_b, got_b, keep_c, send_c, got_c, split,
-     loads, send_sems, recv_sems, halo_sems) = refs
+     loads, send_sems, recv_sems, halo_sems, _) = refs
     seq, head = lax.axis_index("seq"), lax.axis_index("head")
     n_head = lax.axis_size("head")
     core = lax.rem(seq, 2)
     chunks, own, width = act.shape
     half_b, half_w = keep_a.shape[1], keep_b.shape[2]
+    for n in range(3):
+        load[n].start()
     for c in range(chunks):
+        pltpu.make_async_copy(gpre_hbm.at[c], gpre.at[c], loads.at[chunks + c]).start()
+        if c == 0:
+            load[3].start()
         pltpu.make_async_copy(act_hbm.at[c], act.at[c], loads.at[c]).start()
-        pltpu.make_async_copy(gpre_hbm.at[c], gpre.at[c], loads.at[chunks + c]).start()
+    load[5].start()
+    load[4].start()
 
     barrier = pltpu.get_barrier_semaphore()
     pl.semaphore_signal(barrier, inc=1, device_id={"seq": seq ^ OTHER_CORE}, device_id_type=MESH)
@@ -923,12 +978,12 @@
     pl.semaphore_wait(barrier, 1 + (head > 0).astype(jnp.int32) + (head < n_head - 1).astype(jnp.int32))
 
     up = pltpu.make_async_remote_copy(
-        src_ref=gs.at[pl.ds(own - MAXLEN, MAXLEN)], dst_ref=gsw.at[pl.ds(0, MAXLEN)],
+        src_ref=gs_hbm.at[pl.ds(own - MAXLEN, MAXLEN)], dst_ref=gsw.at[pl.ds(0, MAXLEN)],
         send_sem=halo_sems.at[0], recv_sem=halo_sems.at[1],
         device_id={"head": lax.rem(head + 1, n_head)}, device_id_type=MESH,
     )
     down = pltpu.make_async_remote_copy(
-        src_ref=gs.at[pl.ds(0, MAXLEN)], dst_ref=gsw.at[pl.ds(own + MAXLEN, MAXLEN)],
+        src_ref=gs_hbm.at[pl.ds(0, MAXLEN)], dst_ref=gsw.at[pl.ds(own + MAXLEN, MAXLEN)],
         send_sem=halo_sems.at[2], recv_sem=halo_sems.at[3],
         device_id={"head": lax.rem(head + n_head - 1, n_head)}, device_id_type=MESH,
     )
@@ -941,8 +996,6 @@
     @pl.when(head > 0)
     def _():
         down.start()
-
-    stay.start()
 
     def to_core(send, got, first, n):
         return pltpu.make_async_remote_copy(
@@ -961,9 +1014,13 @@
             keep[g] = mine[g]
             send[g] = theirs[g]
 
+    put(dot(cls[...], gpool[...], TN), half_w, keep_c.at[1], send_c.at[1])
+    load[0].wait()
+    load[1].wait()
+    put(dot(ctx[...], gattn[...], TN), half_w, keep_c.at[0], send_c.at[0])
+    load[2].wait()
     mid_t[...] = mid[...].T
-    put(dot(ctx[...], gattn[...], TN), half_w, keep_c.at[0], send_c.at[0])
-    put(dot(cls[...], gpool[...], TN), half_w, keep_c.at[1], send_c.at[1])
+    load[3].wait()
 
     def chunk(c, carry):
         pltpu.make_async_copy(gpre_hbm.at[c], gpre.at[c], loads.at[chunks + c]).wait()
@@ -986,6 +1043,9 @@
 
     lax.fori_loop(0, chunks, chunk, 0)
 
+    load[5].wait()
+    stay.start()
+    load[4].wait()
     tok_t[...] = tok[...].T
 
     place = seq // 2
@@ -1001,6 +1061,7 @@
                     h * quarter : (h + 1) * quarter
                 ].astype(outs[r].dtype)
     copy_a(chunks - 1).start()
+    store[7].start()
 
     def sum_b(c, carry):
         copy_b(c).wait_recv()
@@ -1015,18 +1076,23 @@
         return carry
 
     lax.fori_loop(0, chunks, sum_b, 0)
+    for n in (5, 6, 4):
+        store[n].start()
     for c in range(chunks):
         copy_a(c).wait_recv()
     for r in turns:
         total = keep_a[place ^ r].astype(f32) + got_a[place ^ r].astype(f32)
         for h in range(4):
             outs[r][h, :rows_a, :] = total[h * rows_a : (h + 1) * rows_a].astype(outs[r].dtype)
+        store[r].start()
     for c in range(chunks):
         copy_a(c).wait_send()
         copy_b(c).wait_send()
     for n in range(2):
         copy_c(n).wait_send()
     stay.wait()
+    for copy in store:
+        copy.wait()
 
     @pl.when(head < n_head - 1)
     def _():
@@ -1046,15 +1112,19 @@
     shape = jax.ShapeDtypeStruct
     vmem, hbm = pl.BlockSpec(memory_space=pltpu.VMEM), pl.BlockSpec(memory_space=pl.ANY)
     kinds = (f32, bf16, bf16, bf16)
-    return pl.pallas_call(
+    outs = (
+        [shape((4, half_b // 4 + half_w // 2, width), k) for k in kinds]
+        + [shape((4, half_w // 4, chunks * width), k) for k in kinds[:2]]
+        + [shape((2, 4, half_w // 4, chunks * width), bf16), shape((width, own), bf16)]
+    )
+    held = (ctx, gattn, mid, gffn, tok, gs)
+    gsw, *pieces, tok_t = pl.pallas_call(
         grads_kernel,
-        in_specs=[hbm, hbm] + [vmem] * 8,
-        out_specs=[hbm] + [vmem] * 8,
-        out_shape=[shape((window, width + SIDE), bf16), shape((width, own), bf16)]
-        + [shape((4, half_b // 4 + half_w // 2, width), k) for k in kinds]
-        + [shape((4, half_w // 4, chunks * width), k) for k in kinds[:2]]
-        + [shape((2, 4, half_w // 4, chunks * width), bf16)],
-        scratch_shapes=[
+        in_specs=[hbm] * 8 + [vmem] * 2,
+        out_specs=[hbm] * 9,
+        out_shape=[shape((window, width + SIDE), bf16)] + outs,
+        scratch_shapes=[pltpu.VMEM(o.shape, o.dtype) for o in [*outs, *held]]
+        + [
             pltpu.VMEM((chunks, own, width), bf16),
             pltpu.VMEM((chunks, own, width), bf16),
             pltpu.VMEM((width, own), bf16),
@@ -1068,28 +1138,30 @@
             pltpu.SemaphoreType.DMA((2 * chunks + 2,)),
             pltpu.SemaphoreType.DMA((2 * chunks + 2,)),
             pltpu.SemaphoreType.DMA((5,)),
+            pltpu.SemaphoreType.DMA((14,)),
         ],
         compiler_params=pltpu.CompilerParams(
-            vmem_limit_bytes=60 * 2**20, collective_id=0, has_side_effects=True
+            vmem_limit_bytes=62 * 2**20, collective_id=0, has_side_effects=True
         ),
         cost_estimate=pl.CostEstimate(
             flops=2 * own * width * width * (2 * chunks + 1), bytes_accessed=30 * 2**20, transcendentals=0
         ),
         name="send_grads",
-    )(act, gpre, gs, gffn, mid, ctx, gattn, cls, gpool, tok)
+    )(*held, act, gpre, cls, gpool)
+    return gsw, tok_t, *pieces
 
 
 def finish_kernel(n_parts, *refs):
-    inputs, refs = refs[: 10 + 4 * n_parts], refs[10 + 4 * n_parts :]
-    sends_q = inputs[9 : 9 + n_parts]
+    inputs, refs = refs[:14], refs[14:]
+    sends_q = inputs[9]
     gtok, sum_a, sum_b, sum_out, sum_pool, sum_q, sum_v = refs[:7]
-    n_held = 8 + 3 * n_parts
+    n_held = 11
     held, refs = refs[7 : 7 + n_held], refs[7 + n_held :]
     own_a, near_a, own_b, near_b, vec = held[0], held[1:4], held[4], (held[5], held[6].at[0]), held[7]
-    keeps, vec_parts, parts = (held[8 + n * n_parts : 8 + (n + 1) * n_parts] for n in range(3))
+    keeps, vec_parts, parts = held[8:]
     (w_qkv, all_a, send_a, got_a, all_b, send_b, got_b, got_f, got_q, own_q, send_n, got_n, all_q, send_z, got_z,
      vecs, got_v, loads, send_sems, recv_sems) = refs
-    wanted = inputs[:8] + inputs[9 + n_parts : -1] + (inputs[8], inputs[-1])
+    wanted = inputs[:8] + inputs[10:-1] + (inputs[8], inputs[-1])
     copies = [
         pltpu.make_async_copy(src, dst, loads.at[n])
         for n, (src, dst) in enumerate(zip(wanted, held + (w_qkv, gtok)))
@@ -1112,7 +1184,7 @@
         sends.plan(("a", r), send_a.at[r - 1], got_a.at[r - 1], head=head ^ r)
         sends.plan(("b", r), send_b.at[r - 1], got_b.at[r - 1], seq=seq ^ NEAR[r - 1])
     for p in range(n_parts):
-        sends.plan(("core", p), sends_q[p], got_q.at[p], seq=seq ^ OTHER_CORE)
+        sends.plan(("core", p), sends_q.at[p], got_q.at[p], seq=seq ^ OTHER_CORE)
         for r in line:
             sends.plan(("near", p, r), send_n.at[p, r - 1], got_n.at[p, r - 1], seq=seq ^ NEAR[r - 1])
             sends.plan(("line", p, r), send_z.at[p, r - 1], got_z.at[p, r - 1], head=head ^ r)
@@ -1124,12 +1196,12 @@
     sends.start(*[("core", p) for p in range(n_parts)])
     sends.start("pass")
 
-    for copy in copies[: 8 + 2 * n_parts]:
+    for copy in copies[:10]:
         copy.wait()
     rows_v = vec.shape[0]
     vecs[0, :rows_v, :] = vec[...]
     for p in range(n_parts):
-        vecs[0, rows_v:, p * cols : (p + 1) * cols] = vec_parts[p][...]
+        vecs[0, rows_v:, p * cols : (p + 1) * cols] = vec_parts[p]
     for h in range(4):
         all_a[h] = (own_a[h] + near_a[0][h].astype(f32)) + (
             near_a[1][h].astype(f32) + near_a[2][h].astype(f32)
@@ -1146,10 +1218,10 @@
         for r in line:
             for n in range(3):
                 send_n[p, r - 1, n] = (
-                    keeps[p][n, place ^ r].astype(f32) + got_q[p, n, place ^ r].astype(f32)
+                    keeps[p, n, place ^ r].astype(f32) + got_q[p, n, place ^ r].astype(f32)
                 ).astype(bf16)
         for n in range(3):
-            own_q[p, n] = keeps[p][n, place].astype(f32) + got_q[p, n, place].astype(f32)
+            own_q[p, n] = keeps[p, n, place].astype(f32) + got_q[p, n, place].astype(f32)
         if p == 0:
             sends.start(*[("a", r) for r in line])
         else:
@@ -1164,12 +1236,12 @@
         )
     for r in line:
         send_b[r - 1] = all_b[place ^ r].astype(bf16)
-    for copy in copies[8 + 2 * n_parts :]:
+    for copy in copies[10:]:
         copy.wait()
 
     def back(n, carry):
         here = pl.ds(pl.multiple_of(n * width, width), width)
-        gtok[...] += dot(jnp.concatenate([p[n] for p in parts], axis=1), w_qkv[:, here], NT)
+        gtok[...] += dot(jnp.concatenate([parts[p, n] for p in range(n_parts)], axis=1), w_qkv[:, here], NT)
 
         @pl.when(n == 0)
         def _():
@@ -1220,18 +1292,18 @@
     own, width = gar.shape
     half_w = width // 8
     quarter = half_w // 4
-    n_parts = len(parts)
+    n_parts = parts[0].shape[0]
     cols = width // n_parts
     rows_z, ff = a[0].shape[1], b[0].shape[2]
     n_vec = vec.shape[0] + 8
     shape = jax.ShapeDtypeStruct
     vmem, hbm = pl.BlockSpec(memory_space=pltpu.VMEM), pl.BlockSpec(memory_space=pl.ANY)
     n_copies = 6 + 7 * n_parts + 7 + 1
-    grads, keeps, sends, sums = ([p[n] for p in parts] for n in range(4))
-    held = [*a, *b, vec, *keeps, *sums, *grads]
+    grads, keeps, sends, sums = parts
+    held = [*a, *b, vec, keeps, sums, grads]
     return pl.pallas_call(
         functools.partial(finish_kernel, n_parts),
-        in_specs=[hbm] * (10 + 4 * n_parts),
+        in_specs=[hbm] * 14,
         out_specs=[vmem] * 7,
         out_shape=[
             shape((own, width), f32),
@@ -1266,13 +1338,13 @@
             pltpu.SemaphoreType.DMA((n_copies,)),
         ],
         compiler_params=pltpu.CompilerParams(
-            vmem_limit_bytes=56 * 2**20, collective_id=1, has_side_effects=True
+            vmem_limit_bytes=62 * 2**20, collective_id=1, has_side_effects=True
         ),
         cost_estimate=pl.CostEstimate(
             flops=12 * own * width * width, bytes_accessed=12 * 2**20, transcendentals=0
         ),
         name="finish",
-    )(*a, *b, vec, w_qkv, *sends, *keeps, *sums, *grads, gar)
+    )(*a, *b, vec, w_qkv, sends, keeps, sums, grads, gar)
 
 
 def halo(rows, left_axis, n_head):
@@ -1360,9 +1432,8 @@
     window = own + 2 * MAXLEN
     group = own * n_head
 
-    small = jnp.stack(
-        [b_out, gain_attn, shift_attn, b_back, gain_ffn, shift_ffn, b_pool, b_query, b_value]
-    )
+    vectors = (b_out, gain_attn, shift_attn, b_back, gain_ffn, shift_ffn, b_pool, b_query, b_value)
+    small = jnp.concatenate([*vectors, jnp.zeros((-9 * width % 1024,), f32)]).reshape(1, -1)
     if (n_seq, n_head) == (8, 4):
         qkv, hot, mask, bounds, seqs_of = front(tokens, w_qkv, small, lengths, labels)
     else:
@@ -1411,21 +1482,15 @@
         2 * fold_of(width // PAIR, 3), head_index.reshape(1), w_in, w_back, w_pool, tokens, context, lse,
         cotangent, w_out, b_in.reshape(1, -1), w_class.T, small, seqs_of,
     )
-    pairs = width // PAIR
-    fold = fold_of(pairs, 2)
-    parts = pairs // fold
-    gqkv = []
     if (n_seq, n_head) == (8, 4):
         grads_w, tok_t, *pieces = send_grads(act, gpre, gs, gffn, mid, context, gattn, cls, gpool, tokens)
         to = lambda v, axis, count, x: lax.ppermute(v, axis, [(i, i ^ x) for i in range(count)])
         a = [pieces[0]] + [to(pieces[r], "seq", 8, NEAR[r - 1]) for r in (1, 2, 3)]
         b = [pieces[4], to(pieces[5], "head", 4, 1), to(pieces[6], "head", 4, 2)]
-        for part in range(parts):
-            gqkv.append(attend_back(part, fold, bounds, qkv, grads_w, hot, mask, own, (tok_t, core)))
+        gqkv = attend_back(bounds, qkv, grads_w, hot, mask, own, (tok_t, core))
         grad_tokens, sum_wback, sum_win, sum_wout, sum_pool, sum_wqkv, summed = finish(
             gar, w_qkv, vec, gqkv, a, b
         )
-        vectors, vectors_qkv = summed[: vec.shape[0]], summed[vec.shape[0] :]
     else:
         grads_w = halo(gs, "head", n_head)
 
@@ -1434,15 +1499,8 @@
         first = Sums(
             [pieces[0:2], pieces[2:4], pieces[4:6]], orders_all, n_seq, n_head, vec
         )
-        for part in range(parts):
-            gqkv.append(attend_back(part, fold, bounds, qkv, grads_w, hot, mask, own))
-            bounds = after(bounds, gqkv[-1][0, :8, :128])
-            if part + 1 < parts:
-                first.split()
-                sums = lax.optimization_barrier(tuple(first.sent) + (bounds, first.vectors))
-                first.sent, bounds, first.vectors = list(sums[:3]), sums[3], sums[4]
-                first.send()
-        last_out = last_layer(core, n_seq, tokens, gar, w_qkv, gqkv)
+        gqkv = attend_back(bounds, qkv, grads_w, hot, mask, own)
+        last_out = last_layer(core, n_seq, tokens, gar, w_qkv, list(gqkv))
         grad_tokens, vec_qkv = last_out[:2]
         last = Sums(
             [last_out[2:4], last_out[4:6], last_out[6:8]], orders_all, n_seq, n_head, vec_qkv
@@ -1452,19 +1510,20 @@
         sum_q, sum_k, sum_v = last.rest()
         sum_wqkv = jnp.concatenate([sum_q, sum_k, sum_v], axis=1)
 
-        vectors, vectors_qkv = first.vectors, last.vectors
+        summed = jnp.concatenate([first.vectors, last.vectors])
     size = width // shards
-    mine = lax.dynamic_slice_in_dim(vectors, shard * size, size, 1)
-    mine_qkv = lax.dynamic_slice_in_dim(vectors_qkv, shard * size, size, 1)
     chunks = w_in.shape[1] // width
     n_class = w_class.shape[1]
-    grad_bin = lax.dynamic_slice_in_dim(
-        vectors[8 : 8 + chunks].reshape(-1), shard * size * chunks, size * chunks, 0
-    )
+    n_vec = vec.shape[0]
+    mine = lax.dynamic_slice(summed, (0, shard * size), (summed.shape[0], size))
+    row_shards = shards // chunks
+    grad_bin = lax.dynamic_slice(
+        summed, (8 + shard // row_shards, shard % row_shards * (size * chunks)), (1, size * chunks)
+    )[0]
     grad_class = mine[8 + chunks : 8 + chunks + n_class].T
-    entropy_mean = vectors[7, 0] / (n_seq * labels.shape[1])
+    entropy_mean = summed[7, 0] / (n_seq * labels.shape[1])
     return (
-        output, grad_tokens, sum_wqkv, mine_qkv[0], mine_qkv[2], sum_wout, mine[0], mine[1], mine[2],
+        output, grad_tokens, sum_wqkv, mine[n_vec], mine[n_vec + 2], sum_wout, mine[0], mine[1], mine[2],
         sum_win, grad_bin, sum_wback, mine[3], mine[4], mine[5], sum_pool, mine[6], grad_class,
         entropy_mean,
     )

time: 273 us -> 251 us (0.919); the launches traced: 270 us -> 251 us
  Pallas kernels: 231 us -> 221 us
  local copies, waits for them, and re-layouts: 30.8 us -> 20.9 us
    pallas_call x4 -> x2, Pallas kernels: 85.8 us -> 75.9 us  [the longest x1 50.5 us: attend_back(): pl.pallas_call(functools.partial(attend_back_kernel, (6 * fold, 6 * pairs...]
    another operation x10 -> x0, local copies, waits for them, and re-layouts: 6.27 us -> none  [local(): jnp.stack([b_out, gain_attn, shift_attn, b_back, gain_ffn, shift_ffn, b_p...]
    pallas_call x1, Pallas kernels: 22.2 us -> 25.9 us  [attend(): pl.pallas_call(attend_kernel, grid_spec=pltpu.PrefetchScalarGridSpec(num_...]
    pallas_call x1, Pallas kernels: 59.4 us -> 55.8 us  [finish(): pl.pallas_call(functools.partial(finish_kernel, n_parts), in_specs=[hbm]...]
    unnamed x44 -> x33, local copies, waits for them, and re-layouts: 19 us -> 15.5 us
  transfers between devices with their start and end apart: 5 -> 5, of which waited for: 0 -> 0; matrix products, arithmetic and copies ran while one was open for 0% -> 0% of each run, Pallas kernels for 19% -> 20%
where the time goes in v1:
time: 251 us
  Pallas kernels  221 us (88%)
  local copies, waits for them, and re-layouts  20.9 us (8%)
  starting transfers between devices  6.39 us (3%)
  between operations  2.58 us (1%)
    pallas_call x1, Pallas kernels, finish(): pl.pallas_call(functools.partial(finish_kernel, n_parts), in_specs=[hbm]...  55.8 us
    pallas_call x1, Pallas kernels, attend_back(): pl.pallas_call(functools.partial(attend_back_kernel, (6 * fold, 6 * pairs...  50.5 us
    pallas_call x1, Pallas kernels, middle_layer(): pl.pallas_call(functools.partial(middle_kernel, heads_part), in_specs=[pl...  36.2 us
    pallas_call x1, Pallas kernels, front(): pl.pallas_call(front_kernel, in_specs=[vmem, hbm, vmem, vmem, vmem], out_...  27.5 us
    pallas_call x1, Pallas kernels, attend(): pl.pallas_call(attend_kernel, grid_spec=pltpu.PrefetchScalarGridSpec(num_...  25.9 us
    pallas_call x1, Pallas kernels, send_grads(): pl.pallas_call(grads_kernel, in_specs=[hbm] * 8 + [vmem] * 2, out_specs=[...  25.4 us
    unnamed x33, local copies, waits for them, and re-layouts  15.5 us
    ppermute x5, starting transfers between devices, local(): lax.ppermute(v, axis, [(i, i ^ x) for i in range(count)])  6.39 us
  transfers between devices with their start and end apart: 5, of which 0 were waited for; matrix products, arithmetic and copies ran while one was open for 0% of the time, Pallas kernels for 20%

profile of v1, /device:TPU:0, one launch (start us, length us, event | category | flops | bytes accessed | tf_op | source)
XLA Modules:
  0.0 251.3 jit_solution(1824200056317241354)
XLA Ops:
  0.7 0.7 constant_dynamic-update-slice_fusion.9
  1.4 0.7 constant_dynamic-update-slice_fusion.8
  2.1 0.7 constant_dynamic-update-slice_fusion.7
  2.7 0.7 constant_dynamic-update-slice_fusion.6
  3.4 0.7 constant_dynamic-update-slice_fusion.5
  4.1 0.7 constant_dynamic-update-slice_fusion.4
  4.8 0.7 constant_dynamic-update-slice_fusion.3
  5.5 0.7 constant_dynamic-update-slice_fusion.2
  6.2 0.7 constant_dynamic-update-slice_fusion.1
  6.9 0.6 copy-done.8
  7.5 27.5 %front.1 = (bf16[1792,2304]{1,0:T(8,128)(2,1)}, bf16[1792,128]{1,0:T(8,128)(2,1)}, bf16[1920,128]{1,0:T(8,128)(2,1)}, s32[16,128]{1,0:T(8,128)}, s32[32,128]{1,0:T(8,128)}) custom-call(bf16[768,768]{1,0:T(8,128)(2,1)} %tok_hbm.1, bf16[768,2304]{1,0:T(8,128)(2,1)} %refs_8_.1, f32[1,7168]{1,0:T(1,128)} %bitcast.28, s32[1,24]{1,0:T(1,128)} %lens.1, s32[1,24]{1,0:T(1,128)} %labels.1), custom_call_target="tpu_custom_call" | custom-call | flops 6341787648 | bytes 16777216 | tf_op jit(solution)/shard_map/front/pallas_call | solution.py:902
  35.1 25.9 %attend.1 = (bf16[768,768]{1,0:T(8,128)(2,1)}, f32[16,768]{1,0:T(8,128)}) custom-call(s32[16,128]{1,0:T(8,128)} %get-tuple-element.57.bounds, bf16[1792,2304]{1,0:T(8,128)(2,1)} %get-tuple-element.58.q_ref.k_ref.v_ref, bf16[1792,2304]{1,0:T(8,128)(2,1)} %get-tuple-element.58.q_ref.k_ref.v_ref, bf16[1792,2304]{1,0:T(8,128)(2,1)} %get-tuple-element.58.q_ref.k_ref.v_ref, ...), custom_call_target="tpu_custom_call" | custom-call | flops 1415577600 | bytes 8257536 | tf_op jit(solution)/shard_map/attend/pallas_call | solution.py:118
  60.9 36.2 %middle_layer.1 = (bf16[768,768]{1,0:T(8,128)(2,1)}, f32[768,768]{1,0:T(8,128)}, bf16[768,896]{1,0:T(8,128)(2,1)}, bf16[4,768,768]{2,1,0:T(8,128)(2,1)}, bf16[4,...) custom-call(s32[1]{0:T(128)} %bitcast.place, ...), custom_call_target="tpu_custom_call" | custom-call | flops 19931332608 | bytes 31457280 | tf_op jit(solution)/shard_map/middle_layer/pallas_call | solution.py:532
  97.1 25.4 %send_grads.1 = (bf16[1792,896]{1,0:T(8,128)(2,1)}, f32[4,144,768]{2,1,0:T(8,128)}, bf16[4,144,768]{2,1,0:T(8,128)(2,1)}, bf16[4,144,768]{2,1,0:T(8,128)(2,1)}, ...) custom-call(bf16[768,768]{1,0:T(8,128)(2,1)} %get-tuple-element.62.c, ...), custom_call_target="tpu_custom_call" | custom-call | flops 8153726976 | bytes 31457280 | tf_op jit(solution)/shard_map/send_grads/pallas_call | solution.py:1121
  122.6 1.5 collective-permute-start.4
  124.1 0.7 collective-permute-start
  124.7 2.0 collective-permute-start.1
  126.8 1.5 collective-permute-start.2
  128.2 0.7 collective-permute-start.3
  129.0 50.5 %attend_back.1 = (bf16[3,3,768,256]{3,2,1,0:T(8,128)(2,1)}, bf16[3,3,4,96,256]{4,3,2,1,0:T(8,128)(2,1)}, bf16[3,3,4,96,256]{4,3,2,1,0:T(8,128)(2,1)}, f32[3,8,256]{2,1,0:T(8,128)}) custom-call(s32[16,128]{1,0:T(8,128)} %get-tuple-element.57.bounds, bf16[1792,2304]{1,0:T(8,128)(2,1)} %get-tuple-element.58.q_ref.k_ref.v_ref, ...), custom_call_target="tpu_custom_call" | custom-call | flops 8493465600 | bytes 11010048 | tf_op jit(solution)/shard_map/attend_back/pallas_call | solution.py:266
  179.5 0.0 collective-permute-done.3.refs_5_
  179.5 0.0 copy-start.2
  179.5 0.0 collective-permute-done.refs_1_
  179.5 0.0 copy-start.1
  179.5 0.0 collective-permute-done.1.refs_2_
  179.5 0.0 collective-permute-done.2.refs_3_
  179.5 0.0 collective-permute-done.4.refs_6_
  179.6 0.9 copy-done.1
  180.5 0.2 copy-done.2
  180.6 0.9 copy-done
  181.5 55.8 %finish.1 = (f32[768,768]{1,0:T(8,128)}, f32[96,768]{1,0:T(8,128)}, f32[24,3072]{1,0:T(8,128)}, f32[24,768]{1,0:T(8,128)}, f32[24,768]{1,0:T(8,128)}, /*index=5*/f32[24,2304]{1,0:T(8,128)}, f32[32,768]{1,0:T(8,128)}) custom-call(f32[4,144,768]{2,1,0:T(8,128)} %get-tuple-element.73.refs_0_, bf16[4,144,768]{2,1,0:T(8,128)(2,1)} %copy-done.1, ...), custom_call_target="tpu_custom_call" | custom-call | flops 5435817984 | bytes 12582912 | tf_op jit(solution)/shard_map/finish/pallas_call | solution.py:1304
  237.3 1.2 slice.43
  238.5 1.3 dynamic-slice_bitcast_fusion.10
  239.8 1.3 dynamic-slice_bitcast_fusion
  241.8 1.6 dynamic-slice_bitcast_fusion.1
  243.4 0.0 copy-start.7
  243.4 0.0 copy-start.4
  243.4 0.0 copy-start.3
  243.4 3.3 %copy.55 = f32[768,768]{1,0:T(8,128)} copy(f32[768,768]{1,0:T(8,128)} %get-tuple-element.124) | data formatting | bytes 4718592
  246.7 0.0 copy-done.5
  246.7 0.7 copy.56
  247.4 0.0 copy-done.7
  247.4 0.6 copy.57
  248.1 0.0 copy-done.4
  248.1 0.7 copy.58
  248.8 0.0 copy-done.3
  248.8 0.7 copy.59
  249.5 0.6 copy.60
  (7 shorter events, 0.0 us)
Async XLA Ops:
  6.9 0.6 copy-start.8
  122.6 57.0 %collective-permute-start.4 = (bf16[2,4,24,3072]{3,2,1,0:T(8,128)(2,1)}, bf16[2,4,24,3072]{3,2,1,0:T(8,128)(2,1)S(1)}, u32[]{:S(2)}, u32[]{:S(2)}) collective-permute-start(bf16[2,4,24,3072]{3,2,1,0:T(8,128)(2,1)} %get-tuple-element.79), channel_id=1, source_target_pairs={{0,2},{1,3},{2,0},{3,1},{4,6},{5,7},{6,4},{7,5},{8,10},{9,11},{10,... | collective-permute-start | bytes 3538952 | tf_op jit(solution)/shard_map/ppermute | solution.py:1487
  124.1 55.4 %collective-permute-start = (bf16[4,144,768]{2,1,0:T(8,128)(2,1)}, bf16[4,144,768]{2,1,0:T(8,128)(2,1)S(1)}, u32[]{:S(2)}, u32[]{:S(2)}) collective-permute-start(bf16[4,144,768]{2,1,0:T(8,128)(2,1)} %get-tuple-element.74), channel_id=1, source_target_pairs={{0,8},{4,12},{8,0},{12,4},{16,24},{20,28},{24,16},{28,20},{1,9},{5... | collective-permute-start | bytes 2654216 | tf_op jit(solution)/shard_map/ppermute | solution.py:1487
  124.7 54.8 %collective-permute-start.1 = (bf16[4,144,768]{2,1,0:T(8,128)(2,1)}, bf16[4,144,768]{2,1,0:T(8,128)(2,1)}, u32[]{:S(2)}, u32[]{:S(2)}) collective-permute-start(bf16[4,144,768]{2,1,0:T(8,128)(2,1)} %get-tuple-element.75), channel_id=1, source_target_pairs={{0,16},{4,20},{8,24},{12,28},{16,0},{20,4},{24,8},{28,12},{1,17},{... | collective-permute-start | bytes 2654216 | tf_op jit(solution)/shard_map/ppermute | solution.py:1487
  126.8 52.8 %collective-permute-start.2 = (bf16[4,144,768]{2,1,0:T(8,128)(2,1)}, bf16[4,144,768]{2,1,0:T(8,128)(2,1)}, u32[]{:S(2)}, u32[]{:S(2)}) collective-permute-start(bf16[4,144,768]{2,1,0:T(8,128)(2,1)} %get-tuple-element.76), channel_id=1, source_target_pairs={{0,24},{4,28},{8,16},{12,20},{16,8},{20,12},{24,0},{28,4},{1,25},{... | collective-permute-start | bytes 2654216 | tf_op jit(solution)/shard_map/ppermute | solution.py:1487
  128.2 51.3 %collective-permute-start.3 = (bf16[4,24,3072]{2,1,0:T(8,128)(2,1)}, bf16[4,24,3072]{2,1,0:T(8,128)(2,1)S(1)}, u32[]{:S(2)}, u32[]{:S(2)}) collective-permute-start(bf16[4,24,3072]{2,1,0:T(8,128)(2,1)} %get-tuple-element.78), channel_id=1, source_target_pairs={{0,1},{1,0},{2,3},{3,2},{4,5},{5,4},{6,7},{7,6},{8,9},{9,8},{10,11... | collective-permute-start | bytes 1769480 | tf_op jit(solution)/shard_map/ppermute | solution.py:1487
  179.5 1.1 copy-start.2
  179.5 1.0 copy-start.1
  180.5 1.0 copy-start
  243.4 3.3 %copy-start.5 = (f32[24,2304]{1,0:T(8,128)S(1)}, f32[24,2304]{1,0:T(8,128)}, u32[]{:S(2)}) copy-start(f32[24,2304]{1,0:T(8,128)} %get-tuple-element.125) | copy-start | bytes 663556
  243.4 4.0 %copy-start.7 = (f32[24,768]{1,0:T(8,128)S(1)}, f32[24,768]{1,0:T(8,128)}, u32[]{:S(2)}) copy-start(f32[24,768]{1,0:T(8,128)} %get-tuple-element.128) | copy-start | bytes 221188
  243.4 4.6 %copy-start.4 = (f32[24,3072]{1,0:T(8,128)S(1)}, f32[24,3072]{1,0:T(8,128)}, u32[]{:S(2)}) copy-start(f32[24,3072]{1,0:T(8,128)} %get-tuple-element.132) | copy-start | bytes 884740
  243.4 5.4 %copy-start.3 = (f32[96,768]{1,0:T(8,128)S(1)}, f32[96,768]{1,0:T(8,128)}, u32[]{:S(2)}) copy-start(f32[96,768]{1,0:T(8,128)} %get-tuple-element.134) | copy-start | bytes 884740
  246.7 2.8 %copy-start.6 = (f32[24,768]{1,0:T(8,128)S(1)}, f32[24,768]{1,0:T(8,128)}, u32[]{:S(2)}) copy-start(f32[24,768]{1,0:T(8,128)} %get-tuple-element.138) | copy-start | bytes 221188
